TPU v7x, 256 devices: a whole 4x4x8 slice. The times are simulated.
256 devices in a mesh: blk: 16 (over z, x_hi), leaf: 8 (over y, core), rhs: 2 (over x_lo).
Axes of the slice: x: 4 (x_hi: 2, x_lo: 2; x = x_hi * 2 + x_lo), y: 4, z: 8, core: 2. Of those that a mesh axis runs over, the one named last changes fastest.
Arguments:
- residual: float32 [32, 8, 65536], P('rhs', 'leaf', 'blk'), may hold values from -160 to 160
- points: float32 [3, 8, 65536], P(None, 'leaf', 'blk'), may hold values from -12330 to 12330
- noise: float32 [8, 65536], P('leaf', 'blk'), may hold values from 1 to 2
- block_list: int32 [8, 8, 256], P('leaf'), may hold values from 0 to 1, as said below
Outputs:
- correction: float32 [32, 8, 65536], P('rhs', 'leaf', 'blk')
- new_residual: float32 [32, 8, 65536], P('rhs', 'leaf', 'blk')
- basis: float32 [128, 8, 65536], P('rhs', 'leaf', 'blk')
Inputs may be any that keep to these rules, and one draw needn't show every extreme that they name: The list is symmetric: block_list[t, k, i] == block_list[t, 7 - k, (i + d) mod 256] with d the offset of entry k.
All inputs are finite; a program needn't handle non-finite values.
Results may differ from a plain program's by a relative error of at most 0.007.
Values sent between devices are 32-bit elements; how exact they have to be, the bound alone decides.
A program may use at most 128 MiB of HBM per device.

v0:
```python
import jax
import jax.numpy as jnp
from jax import lax
from jax.sharding import PartitionSpec as P

M = 32
S = 4
BS = 256
REACH = 4
SUPPORT = 1408


centre_shift = 1.5
amplitude = 1.1
exact = lax.Precision.HIGHEST


def extended(x, axes, count, width):
    length = x.shape[1]
    up = [(i, (i + 1) % count) for i in range(count)]
    down = [(j, i) for i, j in up]
    before = lax.ppermute(x[:, length - width :], axes, up)
    after = lax.ppermute(x[:, :width], axes, down)
    return jnp.concatenate([before, x, after], axis=1)


def swap_pair(x, part):
    return lax.ppermute(x, "rhs", [(0, 1), (1, 0)])


def in_order(mine, other, part, axis):
    first = jnp.concatenate([mine, other], axis=axis)
    second = jnp.concatenate([other, mine], axis=axis)
    return jnp.where(part == 0, first, second)


def kernel_tile(near_points, own_points):
    squared = (near_points[0][:, None] - own_points[0][None, :]) ** 2
    squared = squared + (near_points[1][:, None] - own_points[1][None, :]) ** 2
    squared = squared + (near_points[2][:, None] - own_points[2][None, :]) ** 2
    radius = jnp.sqrt(squared) / SUPPORT
    remain = jnp.maximum(1.0 - radius, 0.0)
    return remain * remain * (remain * remain) * (4.0 * radius + 1.0) * (amplitude / SUPPORT)


def band_tiles(points_wide, weights, rows_out):
    width = 2 * REACH + 1
    blocks = points_wide.reshape(3, -1, BS)
    own = blocks[:, REACH : REACH + rows_out]
    near = jnp.stack([blocks[:, k : k + rows_out] for k in range(width)], axis=2)
    tiles = jax.vmap(jax.vmap(kernel_tile, in_axes=(1, None)), in_axes=(1, 1))(near, own)
    return tiles * jnp.transpose(weights)[:, :, None, None]


def band_product(field_wide, tiles, rows_out):
    width = 2 * REACH + 1
    count = field_wide.shape[0]
    blocks = field_wide.reshape(count, -1, BS)
    near = jnp.stack([blocks[:, k : k + rows_out] for k in range(width)], axis=2)
    out = jnp.einsum("mbkq,bkqp->mbp", near, tiles, precision=exact)
    return out.reshape(count, rows_out * BS)


def galerkin(gram, count_points, count_sides):
    normed = gram / count_points
    basis_count = normed.shape[0]
    gram_basis = normed[:basis_count, :basis_count]
    factor_low = jnp.linalg.cholesky(gram_basis)
    inverse_low = lax.linalg.triangular_solve(
        factor_low, jnp.eye(basis_count, dtype=jnp.float32), left_side=True, lower=True
    )
    cross = normed[:basis_count, count_sides:] + centre_shift * gram_basis
    projected = jnp.dot(
        jnp.dot(inverse_low, cross, precision=exact), inverse_low.T, precision=exact
    )
    projected = 0.5 * (projected + projected.T)
    small_side = jnp.dot(inverse_low, gram_basis[:, :count_sides], precision=exact)
    proj_factor = jnp.linalg.cholesky(projected)
    halfway = lax.linalg.triangular_solve(proj_factor, small_side, left_side=True, lower=True)
    coeffs = lax.linalg.triangular_solve(
        proj_factor, halfway, left_side=True, lower=True, transpose_a=True
    )
    combo = jnp.dot(coeffs.T, inverse_low, precision=exact)
    return (inverse_low, combo)


def row_products(rows, cols):
    return lax.dot_general(rows, cols, (((1,), (1,)), ((), ())), precision=exact)


def butterfly_sum(x, axes):
    for axis in axes:
        count = lax.axis_size(axis)
        if count & (count - 1):
            x = lax.psum(x, axis)
            continue
        step = 1
        while step < count:
            x = x + lax.ppermute(x, axis, [(i, i ^ step) for i in range(count)])
            step *= 2
    return x


def local(residual, points, noise, block_list):
    part = lax.axis_index("rhs")
    pairs = lax.axis_size("rhs")
    blk_count = lax.axis_size("blk")
    own = residual[:, 0]
    own_points = points[:, 0]
    length = own.shape[1]
    half = length // pairs
    rim = REACH * BS
    inner = length - rim
    ring_axes = ("blk", "rhs")

    def at(b, j):
        return (b % blk_count) * pairs + j

    same_side = [(at(b, 0), at(b + 1, 0)) for b in range(blk_count)]
    same_side += [(at(b, 1), at(b - 1, 1)) for b in range(blk_count)]
    cross_side = [(at(b, 1), at(b + 1, 0)) for b in range(blk_count)]
    cross_side += [(at(b, 0), at(b - 1, 1)) for b in range(blk_count)]
    from_partner = swap_pair(lax.dynamic_slice_in_dim(own, (1 - part) * rim, inner, 1), part)
    edge_at = (1 - part) * inner
    edge = jnp.concatenate(
        [
            lax.dynamic_slice_in_dim(own, edge_at, rim, 1),
            lax.dynamic_slice_in_dim(own_points, edge_at, rim, 1),
        ],
        axis=0,
    )
    from_same = lax.ppermute(edge, ring_axes, same_side)
    from_cross = lax.ppermute(
        lax.dynamic_slice_in_dim(own, part * inner, rim, 1), ring_axes, cross_side
    )
    sides_here = own.shape[0]
    mine_wide = lax.dynamic_slice_in_dim(own, part * rim, inner, 1)
    points_wide = lax.dynamic_slice_in_dim(own_points, part * rim, inner, 1)
    same_field = from_same[:sides_here]
    same_points = from_same[sides_here:]
    low_first = jnp.concatenate(
        [jnp.concatenate([same_field, mine_wide], 1), jnp.concatenate([from_cross, from_partner], 1)], 0
    )
    high_first = jnp.concatenate(
        [jnp.concatenate([from_partner, from_cross], 1), jnp.concatenate([mine_wide, same_field], 1)], 0
    )
    first_wide = jnp.where(part == 0, low_first, high_first)
    coords_wide = jnp.where(
        part == 0,
        jnp.concatenate([same_points, points_wide], 1),
        jnp.concatenate([points_wide, same_points], 1),
    )
    field = first_wide[:, rim : rim + half]
    nugget = lax.dynamic_slice_in_dim(noise[0], part * half, half, 0)
    own_blocks = half // BS
    ring = lax.axis_size("blk") * pairs
    first_block = (lax.axis_index("blk") * pairs + part) * own_blocks
    listed = block_list[0].astype(jnp.float32)
    nine = jnp.concatenate(
        [listed[:REACH], jnp.ones((1, listed.shape[1]), jnp.float32), listed[REACH:]], axis=0
    )
    margin = S * REACH
    wrapped = jnp.concatenate([nine[:, -margin:], nine, nine[:, :margin]], axis=1)
    powers = [field]
    own_weights = lax.dynamic_slice_in_dim(wrapped, first_block + margin, own_blocks, 1)
    tiles = lax.optimization_barrier(band_tiles(coords_wide, own_weights, own_blocks))
    current = field
    for power_step in range(S):
        widened = first_wide if power_step == 0 else extended(current, ("blk", "rhs"), ring, rim)
        current = band_product(widened, tiles, own_blocks) + (nugget - centre_shift) * current
        powers.append(current)
    flat = jnp.concatenate(powers, axis=0)
    count_points = half * ring * lax.axis_size("leaf")
    gram = butterfly_sum(row_products(flat[: S * M], flat), ("leaf", "blk", "rhs"))
    inverse_low, combo = galerkin(gram, count_points, M)
    first_rows = flat[: S * M]
    image = flat[M:] + centre_shift * first_rows
    correction = jnp.dot(combo, first_rows, precision=exact)
    new_residual = field - jnp.dot(combo, image, precision=exact)
    basis = jnp.dot(inverse_low, first_rows, precision=exact)
    results = []
    for full in (correction, new_residual, basis):
        groups = full.reshape(pairs, -1, half)
        keep = lax.dynamic_index_in_dim(groups, part, 0, False)
        give = lax.dynamic_index_in_dim(groups, 1 - part, 0, False)
        results.append(in_order(keep, swap_pair(give, part), part, 1)[:, None])
    return tuple(results)


def solution(mesh):
    placed = (
        P("rhs", "leaf", "blk"),
        P(None, "leaf", "blk"),
        P("leaf", "blk"),
        P("leaf", None, None),
    )
    return jax.shard_map(
        local,
        mesh=mesh,
        in_specs=placed,
        out_specs=(P("rhs", "leaf", "blk"), P("rhs", "leaf", "blk"), P("rhs", "leaf", "blk")),
        check_vma=False,
    )
```

profile of v0, /device:TPU:16, one launch (start us, length us, event | category | flops | bytes accessed | tf_op | source)
XLA Modules:
  0.0 223.7 jit_solution(17427986495206254736)
XLA Ops:
  1.6 8.1 %collective-permute-start.1 = (f32[16,1024]{1,0:T(8,128)S(1)}, f32[16,1024]{1,0:T(8,128)S(1)}, u32[]{:S(2)}, u32[]{:S(2)}) collective-permute-start(f32[16,1024]{1,0:T(8,128)S(1)} %bitcast.374), channel_id=1, source_target_pairs={{1,16},{17,32},{33,48},{49,64},{65,80},{81,96},{97,112},{113,128},... | collective-permute-start | bytes 196616 | tf_op jit(solution)/shard_map/ppermute | solution.py:133
  13.7 4.4 %collective-permute-done = f32[19,1024]{1,0:T(8,128)S(1)} collective-permute-done((f32[19,1024]{1,0:T(8,128)S(1)}, f32[19,1024]{1,0:T(8,128)S(1)}, u32[]{:S(2)}, u32[]{:S(2)}) %collective-permute-start) | collective-permute-done | bytes 77856 | tf_op jit(solution)/shard_map/ppermute | solution.py:132
  18.4 15.5 %multiply_multiply_fusion = f32[8,9,256,256]{3,2,1,0:T(8,128)S(1)} fusion(f32[8,9]{1,0:T(8,128)S(1)} %copy.49, f32[8,256]{1,0:T(8,128)S(1)} %get-tuple-element.65, f32[8,9,256]{2,1,0:T(8,128)S(1)} %copy.48, f32[8,256]{1,0:T(8,128)S(1)} %get-tuple-element.66, f32[8,9,256]{2,1,0:T(8,128)S(1)} %copy.47, f32[8,256]{1,0:T(8,128)S(1)} %get-tuple-element.64, ...), kind=kLoop, calls=%fused_computation | loop fusion | flops 80216064 | bytes 19120416 | tf_op jit(solution)/shard_map/mul | solution.py:52
  35.2 11.5 %convolution_bitcast_fusion.3 = f32[8,4,8,256]{3,2,1,0:T(8,128)S(1)} fusion(f32[8,9,256,256]{3,2,1,0:T(8,128)S(1)} %multiply_multiply_fusion, f32[32,8,9,256]{3,0,2,1:T(8,128)S(1)} %fusion.8), kind=kOutput, calls=%fused_computation.6 | convolution fusion | flops 1811939328 | bytes 21495808 | tf_op jit(solution)/shard_map/mbkq,bkqp->mbp/dot_general | solution.py:60
  47.6 5.8 %collective-permute-start.4 = (f32[32,1024]{1,0:T(8,128)S(1)}, f32[32,1024]{1,0:T(8,128)S(1)}, u32[]{:S(2)}, u32[]{:S(2)}) collective-permute-start(f32[32,1024]{1,0:T(8,128)S(1)} %get-tuple-element.52), channel_id=1, source_target_pairs={{1,0},{16,1},{17,16},{32,17},{33,32},{48,33},{49,48},{64,49},{65,6... | collective-permute-start | bytes 393224 | tf_op jit(solution)/shard_map/ppermute | solution.py:23
  57.1 11.5 %convolution_bitcast_fusion.2 = f32[8,4,8,256]{3,2,1,0:T(8,128)S(1)} fusion(f32[8,9,256,256]{3,2,1,0:T(8,128)S(1)} %multiply_multiply_fusion, f32[32,8,9,256]{3,0,2,1:T(8,128)S(1)} %fusion.36), kind=kOutput, calls=%fused_computation.5 | convolution fusion | flops 1811939328 | bytes 21495808 | tf_op jit(solution)/shard_map/mbkq,bkqp->mbp/dot_general | solution.py:60
  69.7 5.8 %collective-permute-start.6 = (f32[32,1024]{1,0:T(8,128)S(1)}, f32[32,1024]{1,0:T(8,128)S(1)}, u32[]{:S(2)}, u32[]{:S(2)}) collective-permute-start(f32[32,1024]{1,0:T(8,128)S(1)} %get-tuple-element.50), channel_id=1, source_target_pairs={{1,0},{16,1},{17,16},{32,17},{33,32},{48,33},{49,48},{64,49},{65,6... | collective-permute-start | bytes 393224 | tf_op jit(solution)/shard_map/ppermute | solution.py:23
  75.5 2.9 %collective-permute-done.5 = f32[32,1024]{1,0:T(8,128)S(1)} collective-permute-done((f32[32,1024]{1,0:T(8,128)S(1)}, f32[32,1024]{1,0:T(8,128)S(1)}, u32[]{:S(2)}, u32[]{:S(2)}) %collective-permute-start.5) | collective-permute-done | bytes 131104 | tf_op jit(solution)/shard_map/ppermute | solution.py:22
  79.6 11.5 %convolution_bitcast_fusion.1 = f32[8,4,8,256]{3,2,1,0:T(8,128)S(1)} fusion(f32[8,9,256,256]{3,2,1,0:T(8,128)S(1)} %multiply_multiply_fusion, f32[32,8,9,256]{3,0,2,1:T(8,128)S(1)} %fusion.27), kind=kOutput, calls=%fused_computation.4 | convolution fusion | flops 1811939328 | bytes 21495808 | tf_op jit(solution)/shard_map/mbkq,bkqp->mbp/dot_general | solution.py:60
  92.4 5.5 %collective-permute-start.8 = (f32[32,1024]{1,0:T(8,128)S(1)}, f32[32,1024]{1,0:T(8,128)S(1)}, u32[]{:S(2)}, u32[]{:S(2)}) collective-permute-start(f32[32,1024]{1,0:T(8,128)S(1)} %get-tuple-element.48), channel_id=1, source_target_pairs={{1,0},{16,1},{17,16},{32,17},{33,32},{48,33},{49,48},{64,49},{65,6... | collective-permute-start | bytes 393224 | tf_op jit(solution)/shard_map/ppermute | solution.py:23
  97.9 2.9 %collective-permute-done.7 = f32[32,1024]{1,0:T(8,128)S(1)} collective-permute-done((f32[32,1024]{1,0:T(8,128)S(1)}, f32[32,1024]{1,0:T(8,128)S(1)}, u32[]{:S(2)}, u32[]{:S(2)}) %collective-permute-start.7) | collective-permute-done | bytes 131104 | tf_op jit(solution)/shard_map/ppermute | solution.py:22
  102.0 11.5 %convolution_bitcast_fusion = f32[8,4,8,256]{3,2,1,0:T(8,128)S(1)} fusion(f32[8,9,256,256]{3,2,1,0:T(8,128)S(1)} %multiply_multiply_fusion, f32[32,8,9,256]{3,0,2,1:T(8,128)S(1)} %fusion.18), kind=kOutput, calls=%fused_computation.3 | convolution fusion | flops 1811939328 | bytes 21495808 | tf_op jit(solution)/shard_map/mbkq,bkqp->mbp/dot_general | solution.py:60
  117.8 3.2 %collective-permute-done.10 = f32[128,160]{0,1:T(8,128)S(1)} collective-permute-done((f32[128,160]{0,1:T(8,128)S(1)}, f32[128,160]{0,1:T(8,128)S(1)}, u32[]{:S(2)}, u32[]{:S(2)}) %collective-permute-start.10) | collective-permute-done | bytes 81952 | tf_op jit(solution)/shard_map/ppermute | solution.py:99
  121.4 5.6 %collective-permute-done.11 = f32[128,160]{0,1:T(8,128)S(1)} collective-permute-done((f32[128,160]{0,1:T(8,128)S(1)}, f32[128,160]{0,1:T(8,128)S(1)}, u32[]{:S(2)}, u32[]{:S(2)}) %collective-permute-start.11) | collective-permute-done | bytes 81952 | tf_op jit(solution)/shard_map/ppermute | solution.py:99
  127.1 5.9 %collective-permute-done.12 = f32[128,160]{0,1:T(8,128)S(1)} collective-permute-done((f32[128,160]{0,1:T(8,128)S(1)}, f32[128,160]{0,1:T(8,128)S(1)}, u32[]{:S(2)}, u32[]{:S(2)}) %collective-permute-start.12) | collective-permute-done | bytes 81952 | tf_op jit(solution)/shard_map/ppermute | solution.py:99
  133.2 4.5 %collective-permute-done.13 = f32[128,160]{0,1:T(8,128)S(1)} collective-permute-done((f32[128,160]{0,1:T(8,128)S(1)}, f32[128,160]{0,1:T(8,128)S(1)}, u32[]{:S(2)}, u32[]{:S(2)}) %collective-permute-start.13) | collective-permute-done | bytes 81952 | tf_op jit(solution)/shard_map/ppermute | solution.py:99
  137.8 7.1 %collective-permute-done.14 = f32[128,160]{0,1:T(8,128)S(1)} collective-permute-done((f32[128,160]{0,1:T(8,128)S(1)}, f32[128,160]{0,1:T(8,128)S(1)}, u32[]{:S(2)}, u32[]{:S(2)}) %collective-permute-start.14) | collective-permute-done | bytes 81952 | tf_op jit(solution)/shard_map/ppermute | solution.py:99
  146.1 7.3 %collective-permute-done.15 = f32[128,160]{0,1:T(8,128)S(1)} collective-permute-done((f32[128,160]{0,1:T(8,128)S(1)}, f32[128,160]{0,1:T(8,128)S(1)}, u32[]{:S(2)}, u32[]{:S(2)}) %collective-permute-start.15) | collective-permute-done | bytes 81952 | tf_op jit(solution)/shard_map/ppermute | solution.py:99
  153.5 4.4 %collective-permute-done.16 = f32[128,160]{0,1:T(8,128)S(1)} collective-permute-done((f32[128,160]{0,1:T(8,128)S(1)}, f32[128,160]{0,1:T(8,128)S(1)}, u32[]{:S(2)}, u32[]{:S(2)}) %collective-permute-start.16) | collective-permute-done | bytes 81952 | tf_op jit(solution)/shard_map/ppermute | solution.py:99
  158.1 11.7 %cholesky.44 = f32[128,128]{1,0:T(8,128)S(1)} custom-call(f32[128,128]{1,0:T(8,128)S(1)} %fusion.56), custom_call_target="Cholesky" | custom-call | tf_op jit(solution)/shard_map/jit(cholesky)/cholesky | solution.py:68
  171.1 9.8 %custom-call.10 = f32[1,128,128]{1,2,0:T(8,128)S(1)} custom-call(f32[1,128,128]{2,1,0:T(8,128)S(1)} %fusion.45), custom_call_target="InvertDiagBlocksLowerTriangular" | custom-call | tf_op jit(solution)/shard_map/triangular_solve | solution.py:69
  183.2 11.7 %cholesky.55 = f32[128,128]{1,0:T(8,128)S(1)} custom-call(f32[128,128]{1,0:T(8,128)S(1)} %fusion.52), custom_call_target="Cholesky" | custom-call | tf_op jit(solution)/shard_map/jit(cholesky)/cholesky | solution.py:78
  196.3 10.0 %custom-call.11 = f32[1,128,128]{1,2,0:T(8,128)S(1)} custom-call(f32[1,128,128]{2,1,0:T(8,128)S(1)} %fusion.46), custom_call_target="InvertDiagBlocksLowerTriangular" | custom-call | tf_op jit(solution)/shard_map/triangular_solve | solution.py:80
  216.2 4.4 %collective-permute-done.19 = f32[64,2048]{1,0:T(8,128)S(1)} collective-permute-done((f32[64,2048]{1,0:T(8,128)S(1)}, f32[64,2048]{1,0:T(8,128)S(1)}, u32[]{:S(2)}, u32[]{:S(2)}) %collective-permute-start.19) | collective-permute-done | bytes 524320 | tf_op jit(solution)/shard_map/ppermute | solution.py:28
  (174 shorter events, 39.1 us)
Async XLA Ops:
  0.6 9.1 %copy-start = (f32[3,1,4096]{2,1,0:T(1,128)S(1)}, f32[3,1,4096]{2,1,0:T(1,128)}, u32[]{:S(2)}) copy-start(f32[3,1,4096]{2,1,0:T(1,128)} %param.6) | copy-start | bytes 147460
  1.6 12.1 %collective-permute-start.1 = (f32[16,1024]{1,0:T(8,128)S(1)}, f32[16,1024]{1,0:T(8,128)S(1)}, u32[]{:S(2)}, u32[]{:S(2)}) collective-permute-start(f32[16,1024]{1,0:T(8,128)S(1)} %bitcast.374), channel_id=1, source_target_pairs={{1,16},{17,32},{33,48},{49,64},{65,80},{81,96},{97,112},{113,128},... | collective-permute-start | bytes 196616 | tf_op jit(solution)/shard_map/ppermute | solution.py:133
  9.8 8.3 %collective-permute-start = (f32[19,1024]{1,0:T(8,128)S(1)}, f32[19,1024]{1,0:T(8,128)S(1)}, u32[]{:S(2)}, u32[]{:S(2)}) collective-permute-start(f32[19,1024]{1,0:T(8,128)S(1)} %pad_maximum_fusion.10), channel_id=1, source_target_pairs={{0,16},{16,32},{32,48},{48,64},{64,80},{80,96},{96,112},{112,128},... | collective-permute-start | bytes 233480 | tf_op jit(solution)/shard_map/ppermute | solution.py:132
  11.0 23.0 %collective-permute-start.2 = (f32[16,3072]{1,0:T(8,128)S(1)}, f32[16,3072]{1,0:T(8,128)S(1)}, u32[]{:S(2)}, u32[]{:S(2)}) collective-permute-start(f32[16,3072]{1,0:T(8,128)S(1)} %bitcast.372), channel_id=1, source_target_pairs={{0,1},{1,0},{2,3},{3,2},{4,5},{5,4},{6,7},{7,6},{8,9},{9,8},{10,11... | collective-permute-start | bytes 589832 | tf_op jit(solution)/shard_map/ppermute | solution.py:28
  47.5 8.4 %collective-permute-start.3 = (f32[32,1024]{1,0:T(8,128)S(1)}, f32[32,1024]{1,0:T(8,128)S(1)}, u32[]{:S(2)}, u32[]{:S(2)}) collective-permute-start(f32[32,1024]{1,0:T(8,128)S(1)} %get-tuple-element.51), channel_id=1, source_target_pairs={{0,1},{1,16},{16,17},{17,32},{32,33},{33,48},{48,49},{49,64},{64,6... | collective-permute-start | bytes 393224 | tf_op jit(solution)/shard_map/ppermute | solution.py:22
  47.6 8.3 %collective-permute-start.4 = (f32[32,1024]{1,0:T(8,128)S(1)}, f32[32,1024]{1,0:T(8,128)S(1)}, u32[]{:S(2)}, u32[]{:S(2)}) collective-permute-start(f32[32,1024]{1,0:T(8,128)S(1)} %get-tuple-element.52), channel_id=1, source_target_pairs={{1,0},{16,1},{17,16},{32,17},{33,32},{48,33},{49,48},{64,49},{65,6... | collective-permute-start | bytes 393224 | tf_op jit(solution)/shard_map/ppermute | solution.py:23
  69.4 9.0 %collective-permute-start.5 = (f32[32,1024]{1,0:T(8,128)S(1)}, f32[32,1024]{1,0:T(8,128)S(1)}, u32[]{:S(2)}, u32[]{:S(2)}) collective-permute-start(f32[32,1024]{1,0:T(8,128)S(1)} %get-tuple-element.49), channel_id=1, source_target_pairs={{0,1},{1,16},{16,17},{17,32},{32,33},{33,48},{48,49},{49,64},{64,6... | collective-permute-start | bytes 393224 | tf_op jit(solution)/shard_map/ppermute | solution.py:22
  69.7 8.7 %collective-permute-start.6 = (f32[32,1024]{1,0:T(8,128)S(1)}, f32[32,1024]{1,0:T(8,128)S(1)}, u32[]{:S(2)}, u32[]{:S(2)}) collective-permute-start(f32[32,1024]{1,0:T(8,128)S(1)} %get-tuple-element.50), channel_id=1, source_target_pairs={{1,0},{16,1},{17,16},{32,17},{33,32},{48,33},{49,48},{64,49},{65,6... | collective-permute-start | bytes 393224 | tf_op jit(solution)/shard_map/ppermute | solution.py:23
  91.9 8.9 %collective-permute-start.7 = (f32[32,1024]{1,0:T(8,128)S(1)}, f32[32,1024]{1,0:T(8,128)S(1)}, u32[]{:S(2)}, u32[]{:S(2)}) collective-permute-start(f32[32,1024]{1,0:T(8,128)S(1)} %get-tuple-element.47), channel_id=1, source_target_pairs={{0,1},{1,16},{16,17},{17,32},{32,33},{33,48},{48,49},{49,64},{64,6... | collective-permute-start | bytes 393224 | tf_op jit(solution)/shard_map/ppermute | solution.py:22
  92.4 8.4 %collective-permute-start.8 = (f32[32,1024]{1,0:T(8,128)S(1)}, f32[32,1024]{1,0:T(8,128)S(1)}, u32[]{:S(2)}, u32[]{:S(2)}) collective-permute-start(f32[32,1024]{1,0:T(8,128)S(1)} %get-tuple-element.48), channel_id=1, source_target_pairs={{1,0},{16,1},{17,16},{32,17},{33,32},{48,33},{49,48},{64,49},{65,6... | collective-permute-start | bytes 393224 | tf_op jit(solution)/shard_map/ppermute | solution.py:23
  102.0 11.6 %copy-start.1 = (f32[160,2048]{1,0:T(8,128)S(1)}, f32[160,2048]{1,0:T(8,128)}, u32[]{:S(2)}) copy-start(f32[160,2048]{1,0:T(8,128)} %get-tuple-element.6) | copy-start | bytes 3932164
  115.0 1.4 collective-permute-start.9
  116.4 4.6 %collective-permute-start.10 = (f32[128,160]{0,1:T(8,128)S(1)}, f32[128,160]{0,1:T(8,128)S(1)}, u32[]{:S(2)}, u32[]{:S(2)}) collective-permute-start(f32[128,160]{0,1:T(8,128)S(1)} %add.125), channel_id=1, source_target_pairs={{0,4},{2,6},{4,0},{6,2},{8,12},{10,14},{12,8},{14,10},{1,5},{3,7},... | collective-permute-start | bytes 245768 | tf_op jit(solution)/shard_map/ppermute | solution.py:99
  121.0 6.0 %collective-permute-start.11 = (f32[128,160]{0,1:T(8,128)S(1)}, f32[128,160]{0,1:T(8,128)S(1)}, u32[]{:S(2)}, u32[]{:S(2)}) collective-permute-start(f32[128,160]{0,1:T(8,128)S(1)} %add.126), channel_id=1, source_target_pairs={{0,8},{2,10},{4,12},{6,14},{8,0},{10,2},{12,4},{14,6},{1,9},{3,11}... | collective-permute-start | bytes 245768 | tf_op jit(solution)/shard_map/ppermute | solution.py:99
  127.0 6.0 %collective-permute-start.12 = (f32[128,160]{0,1:T(8,128)S(1)}, f32[128,160]{0,1:T(8,128)S(1)}, u32[]{:S(2)}, u32[]{:S(2)}) collective-permute-start(f32[128,160]{0,1:T(8,128)S(1)} %add.127), channel_id=1, source_target_pairs={{0,16},{16,0},{32,48},{48,32},{64,80},{80,64},{96,112},{112,96},{1... | collective-permute-start | bytes 245768 | tf_op jit(solution)/shard_map/ppermute | solution.py:99
  133.1 4.6 %collective-permute-start.13 = (f32[128,160]{0,1:T(8,128)S(1)}, f32[128,160]{0,1:T(8,128)S(1)}, u32[]{:S(2)}, u32[]{:S(2)}) collective-permute-start(f32[128,160]{0,1:T(8,128)S(1)} %add.128), channel_id=1, source_target_pairs={{0,32},{16,48},{32,0},{48,16},{64,96},{80,112},{96,64},{112,80},{1... | collective-permute-start | bytes 245768 | tf_op jit(solution)/shard_map/ppermute | solution.py:99
  137.7 7.2 %collective-permute-start.14 = (f32[128,160]{0,1:T(8,128)S(1)}, f32[128,160]{0,1:T(8,128)S(1)}, u32[]{:S(2)}, u32[]{:S(2)}) collective-permute-start(f32[128,160]{0,1:T(8,128)S(1)} %add.129), channel_id=1, source_target_pairs={{0,64},{16,80},{32,96},{48,112},{64,0},{80,16},{96,32},{112,48},{1... | collective-permute-start | bytes 245768 | tf_op jit(solution)/shard_map/ppermute | solution.py:99
  145.0 8.4 %collective-permute-start.15 = (f32[128,160]{0,1:T(8,128)S(1)}, f32[128,160]{0,1:T(8,128)S(1)}, u32[]{:S(2)}, u32[]{:S(2)}) collective-permute-start(f32[128,160]{0,1:T(8,128)S(1)} %add.130), channel_id=1, source_target_pairs={{0,128},{16,144},{32,160},{48,176},{64,192},{80,208},{96,224},{112... | collective-permute-start | bytes 245768 | tf_op jit(solution)/shard_map/ppermute | solution.py:99
  153.4 4.5 %collective-permute-start.16 = (f32[128,160]{0,1:T(8,128)S(1)}, f32[128,160]{0,1:T(8,128)S(1)}, u32[]{:S(2)}, u32[]{:S(2)}) collective-permute-start(f32[128,160]{0,1:T(8,128)S(1)} %add.131), channel_id=1, source_target_pairs={{0,1},{1,0},{2,3},{3,2},{4,5},{5,4},{6,7},{7,6},{8,9},{9,8},{10,11... | collective-permute-start | bytes 245768 | tf_op jit(solution)/shard_map/ppermute | solution.py:99
  208.6 5.1 %collective-permute-start.18 = (f32[16,2048]{1,0:T(8,128)S(1)}, f32[16,2048]{1,0:T(8,128)S(1)}, u32[]{:S(2)}, u32[]{:S(2)}) collective-permute-start(f32[16,2048]{1,0:T(8,128)S(1)} %get-tuple-element.44), channel_id=1, source_target_pairs={{0,1},{1,0},{2,3},{3,2},{4,5},{5,4},{6,7},{7,6},{8,9},{9,8},{10,11... | collective-permute-start | bytes 393224 | tf_op jit(solution)/shard_map/ppermute | solution.py:28
  209.2 5.8 %collective-permute-start.17 = (f32[16,2048]{1,0:T(8,128)S(1)}, f32[16,2048]{1,0:T(8,128)S(1)}, u32[]{:S(2)}, u32[]{:S(2)}) collective-permute-start(f32[16,2048]{1,0:T(8,128)S(1)} %get-tuple-element.46), channel_id=1, source_target_pairs={{0,1},{1,0},{2,3},{3,2},{4,5},{5,4},{6,7},{7,6},{8,9},{9,8},{10,11... | collective-permute-start | bytes 393224 | tf_op jit(solution)/shard_map/ppermute | solution.py:28
  211.3 9.3 %collective-permute-start.19 = (f32[64,2048]{1,0:T(8,128)S(1)}, f32[64,2048]{1,0:T(8,128)S(1)}, u32[]{:S(2)}, u32[]{:S(2)}) collective-permute-start(f32[64,2048]{1,0:T(8,128)S(1)} %get-tuple-element.13), channel_id=1, source_target_pairs={{0,1},{1,0},{2,3},{3,2},{4,5},{5,4},{6,7},{7,6},{8,9},{9,8},{10,11... | collective-permute-start | bytes 1572872 | tf_op jit(solution)/shard_map/ppermute | solution.py:28
where the time goes:
time: 228 us; the launch traced here: 224 us
  other arithmetic  71.2 us (31%)
  waiting for transfers between devices  58.6 us (26%)
  matrix products  51.6 us (23%)
  starting transfers between devices  32.8 us (14%)
  local copies, waits for them, and re-layouts  7.58 us (3%)
    dot_general x4, matrix products, band_product(): out = jnp.einsum('mbkq,bkqp->mbp', near, tiles, precision=exact)  46.1 us
    ppermute x8, waiting for transfers between devices, butterfly_sum(): x = x + lax.ppermute(x, axis, [(i, i ^ step) for i in range(count)])  39.4 us
    ppermute x3, starting transfers between devices, extended(): after = lax.ppermute(x[:, :width], axes, down)  17.1 us
    mul x2, other arithmetic, band_tiles(): return tiles * jnp.transpose(weights)[:, :, None, None]  15.6 us
    another operation x3, other arithmetic, galerkin(): factor_low = jnp.linalg.cholesky(gram_basis)  12.4 us
    another operation x3, other arithmetic, galerkin(): proj_factor = jnp.linalg.cholesky(projected)  12.4 us
    another operation x2, other arithmetic, galerkin(): lax.linalg.triangular_solve(proj_factor, halfway, left_side=True, lower=T...  10.7 us
    another operation x2, other arithmetic, galerkin(): lax.linalg.triangular_solve(factor_low, jnp.eye(basis_count, dtype=jnp.fl...  10.5 us
  transfers between devices with their start and end apart: 20, of which 15 were waited for; matrix products, arithmetic and copies ran while one was open for 10% of the time, Pallas kernels for 0%

commit v1 on v0

--- a/solution.py
+++ b/solution.py
@@ -164,11 +164,18 @@
     powers = [field]
     own_weights = lax.dynamic_slice_in_dim(wrapped, first_block + margin, own_blocks, 1)
     tiles = lax.optimization_barrier(band_tiles(coords_wide, own_weights, own_blocks))
-    current = field
-    for power_step in range(S):
-        widened = first_wide if power_step == 0 else extended(current, ("blk", "rhs"), ring, rim)
-        current = band_product(widened, tiles, own_blocks) + (nugget - centre_shift) * current
-        powers.append(current)
+    shift = nugget - centre_shift
+    current = band_product(first_wide, tiles, own_blocks) + shift * field
+    stacked = jnp.zeros((S,) + field.shape, field.dtype).at[0].set(current)
+
+    def power_step(index, carry):
+        stacked, current = carry
+        widened = extended(current, ("blk", "rhs"), ring, rim)
+        current = band_product(widened, tiles, own_blocks) + shift * current
+        return (lax.dynamic_update_index_in_dim(stacked, current, index, 0), current)
+
+    stacked, current = lax.fori_loop(1, S, power_step, (stacked, current))
+    powers = [field] + [stacked[k] for k in range(S)]
     flat = jnp.concatenate(powers, axis=0)
     count_points = half * ring * lax.axis_size("leaf")
     gram = butterfly_sum(row_products(flat[: S * M], flat), ("leaf", "blk", "rhs"))

time: 228 us -> 232 us (1.018)
  waiting for transfers between devices: 58.6 us -> 69 us
  starting transfers between devices: 32.8 us -> 22.6 us
  matrix products: 51.6 us -> 58.5 us
  other arithmetic: 71.2 us -> 67.2 us
    ppermute x3, starting transfers between devices: 17.1 us -> 1.65 us  [extended(): after = lax.ppermute(x[:, :width], axes, down)]
    ppermute x3, waiting for transfers between devices: 0.03 us -> 8.82 us  [extended(): after = lax.ppermute(x[:, :width], axes, down)]
    dot_general x4, matrix products: 46.1 us -> 53.2 us  [band_product(): out = jnp.einsum('mbkq,bkqp->mbp', near, tiles, precision=exact)]
    ppermute x3, starting transfers between devices: 0.83 us -> 4.65 us  [extended(): before = lax.ppermute(x[:, length - width:], axes, up)]
    ppermute x3, waiting for transfers between devices: 8.21 us -> 11.5 us  [extended(): before = lax.ppermute(x[:, length - width:], axes, up)]
    ppermute x4, waiting for transfers between devices: 6.66 us -> 3.65 us  [swap_pair(): return lax.ppermute(x, 'rhs', [(0, 1), (1, 0)])]
    ppermute x1, waiting for transfers between devices: 4.38 us -> 7.35 us  [local(): from_same = lax.ppermute(edge, ring_axes, same_side)]
    while x0 -> x27, local copies, waits for them, and re-layouts: none -> 2.43 us
  transfers between devices with their start and end apart: 20 -> 20, of which waited for: 15 -> 18; matrix products, arithmetic and copies ran while one was open for 10% -> 20% of each run, Pallas kernels for 0% -> 0%
where the time goes in v1:
time: 232 us; the launch traced here: 228 us
  waiting for transfers between devices  69 us (30%)
  other arithmetic  67.2 us (29%)
  matrix products  58.5 us (25%)
  starting transfers between devices  22.6 us (10%)
  local copies, waits for them, and re-layouts  8.66 us (4%)
    dot_general x4, matrix products, band_product(): out = jnp.einsum('mbkq,bkqp->mbp', near, tiles, precision=exact)  53.2 us
    ppermute x8, waiting for transfers between devices, butterfly_sum(): x = x + lax.ppermute(x, axis, [(i, i ^ step) for i in range(count)])  37.2 us
    mul x2, other arithmetic, band_tiles(): return tiles * jnp.transpose(weights)[:, :, None, None]  15.9 us
    another operation x3, other arithmetic, galerkin(): factor_low = jnp.linalg.cholesky(gram_basis)  12.4 us
    another operation x3, other arithmetic, galerkin(): proj_factor = jnp.linalg.cholesky(projected)  12.4 us
    ppermute x3, waiting for transfers between devices, extended(): before = lax.ppermute(x[:, length - width:], axes, up)  11.5 us
    another operation x2, other arithmetic, galerkin(): lax.linalg.triangular_solve(factor_low, jnp.eye(basis_count, dtype=jnp.fl...  10.5 us
    another operation x2, other arithmetic, galerkin(): lax.linalg.triangular_solve(proj_factor, halfway, left_side=True, lower=T...  10.5 us
  transfers between devices with their start and end apart: 20, of which 18 were waited for; matrix products, arithmetic and copies ran while one was open for 20% of the time, Pallas kernels for 0%

profile of v1, /device:TPU:16, one launch (start us, length us, event | category | flops | bytes accessed | tf_op | source)
XLA Modules:
  0.0 228.4 jit_solution(6378661105783159064)
XLA Ops:
  1.6 8.1 %collective-permute-start.3 = (f32[16,1024]{1,0:T(8,128)S(1)}, f32[16,1024]{1,0:T(8,128)S(1)}, u32[]{:S(2)}, u32[]{:S(2)}) collective-permute-start(f32[16,1024]{1,0:T(8,128)S(1)} %bitcast.323), channel_id=1, source_target_pairs={{1,16},{17,32},{33,48},{49,64},{65,80},{81,96},{97,112},{113,128},... | collective-permute-start | bytes 196616 | tf_op jit(solution)/shard_map/ppermute | solution.py:133
  12.0 7.3 %collective-permute-done.2 = f32[19,1024]{1,0:T(8,128)S(1)} collective-permute-done((f32[19,1024]{1,0:T(8,128)S(1)}, f32[19,1024]{1,0:T(8,128)S(1)}, u32[]{:S(2)}, u32[]{:S(2)}) %collective-permute-start.2) | collective-permute-done | bytes 77856 | tf_op jit(solution)/shard_map/ppermute | solution.py:132
  19.7 15.8 %multiply_multiply_fusion = f32[8,9,256,256]{3,2,1,0:T(8,128)S(1)} fusion(f32[8,9]{1,0:T(8,128)S(1)} %copy.43, f32[8,256]{1,0:T(8,128)S(1)} %get-tuple-element.196, f32[8,9,256]{2,1,0:T(8,128)S(1)} %copy.42, f32[8,256]{1,0:T(8,128)S(1)} %get-tuple-element.197, f32[8,9,256]{2,1,0:T(8,128)S(1)} %copy.41, f32[8,256]{1,0:T(8,128)S(1)} %get-tuple-element.195, ...), kind=kLoop, calls=%fused_computation.22 | loop fusion | flops 80216064 | bytes 19120416 | tf_op jit(solution)/shard_map/mul | solution.py:52
  36.1 11.6 %convolution_bitcast_fusion.1 = f32[8,4,8,256]{3,2,1,0:T(8,128)S(1)} fusion(f32[8,9,256,256]{3,2,1,0:T(8,128)S(1)} %multiply_multiply_fusion, f32[32,8,9,256]{3,0,2,1:T(8,128)S(1)} %fusion.17), kind=kOutput, calls=%fused_computation.25 | convolution fusion | flops 1811939328 | bytes 21495808 | tf_op jit(solution)/shard_map/mbkq,bkqp->mbp/dot_general | solution.py:60
  47.9 72.7 %while.18 = (s32[]{:T(128)}, f32[4,32,2048]{2,1,0:T(8,128)S(1)}, f32[32,2048]{1,0:T(8,128)S(1)}, f32[8,9,256,256]{3,2,1,0:T(8,128)}, f32[2048]{0:T(1024)S(1)}, /*index=5*/s32[]{:T(128)}, s32[]{:T(128)}, s32[]{:T(128)}) while((s32[]{:T(128)}, f32[4,32,2048]{2,1,0:T(8,128)S(1)}, f32[32,2048]{1,0:T(8,128)S(1)}, f32[8,9,256,256]{3,2,1,0:T(8,128)}, ...), condition=%wide.region_1.2_spmd, body=%wide.region_0.1_spmd.sunk | while | flops 1812332544 | bytes 36184276 | solution.py:177
  50.2 2.9 %collective-permute-done = f32[32,1024]{1,0:T(8,128)S(1)} collective-permute-done((f32[32,1024]{1,0:T(8,128)S(1)}, f32[32,1024]{1,0:T(8,128)S(1)}, u32[]{:S(2)}, u32[]{:S(2)}) %collective-permute-start) | collective-permute-done | bytes 131104 | tf_op jit(solution)/shard_map/while/body/eval_jaxpr/ppermute | solution.py:23
  53.1 4.7 %collective-permute-done.1 = f32[32,1024]{1,0:T(8,128)S(1)} collective-permute-done((f32[32,1024]{1,0:T(8,128)S(1)}, f32[32,1024]{1,0:T(8,128)S(1)}, u32[]{:S(2)}, u32[]{:S(2)}) %collective-permute-start.1) | collective-permute-done | bytes 131104 | tf_op jit(solution)/shard_map/while/body/eval_jaxpr/ppermute | solution.py:22
  59.1 13.9 %convolution_bitcast_fusion.3 = f32[8,4,8,256]{3,2,1,0:T(8,128)S(1)} fusion(f32[32,8,9,256]{3,0,2,1:T(8,128)S(1)} %fusion.105, f32[8,9,256,256]{3,2,1,0:T(8,128)} %get-tuple-element.282), kind=kOutput, calls=%fused_computation.clone.1 | convolution fusion | flops 1811939328 | bytes 21495808 | tf_op jit(solution)/shard_map/while/body/eval_jaxpr/mbkq,bkqp->mbp/dot_general | solution.py:60
  78.2 3.4 %collective-permute-done.1 = f32[32,1024]{1,0:T(8,128)S(1)} collective-permute-done((f32[32,1024]{1,0:T(8,128)S(1)}, f32[32,1024]{1,0:T(8,128)S(1)}, u32[]{:S(2)}, u32[]{:S(2)}) %collective-permute-start.1) | collective-permute-done | bytes 131104 | tf_op jit(solution)/shard_map/while/body/eval_jaxpr/ppermute | solution.py:22
  82.8 13.9 %convolution_bitcast_fusion.3 = f32[8,4,8,256]{3,2,1,0:T(8,128)S(1)} fusion(f32[32,8,9,256]{3,0,2,1:T(8,128)S(1)} %fusion.105, f32[8,9,256,256]{3,2,1,0:T(8,128)} %get-tuple-element.282), kind=kOutput, calls=%fused_computation.clone.1 | convolution fusion | flops 1811939328 | bytes 21495808 | tf_op jit(solution)/shard_map/while/body/eval_jaxpr/mbkq,bkqp->mbp/dot_general | solution.py:60
  101.9 3.4 %collective-permute-done.1 = f32[32,1024]{1,0:T(8,128)S(1)} collective-permute-done((f32[32,1024]{1,0:T(8,128)S(1)}, f32[32,1024]{1,0:T(8,128)S(1)}, u32[]{:S(2)}, u32[]{:S(2)}) %collective-permute-start.1) | collective-permute-done | bytes 131104 | tf_op jit(solution)/shard_map/while/body/eval_jaxpr/ppermute | solution.py:22
  106.5 13.9 %convolution_bitcast_fusion.3 = f32[8,4,8,256]{3,2,1,0:T(8,128)S(1)} fusion(f32[32,8,9,256]{3,0,2,1:T(8,128)S(1)} %fusion.105, f32[8,9,256,256]{3,2,1,0:T(8,128)} %get-tuple-element.282), kind=kOutput, calls=%fused_computation.clone.1 | convolution fusion | flops 1811939328 | bytes 21495808 | tf_op jit(solution)/shard_map/while/body/eval_jaxpr/mbkq,bkqp->mbp/dot_general | solution.py:60
  125.4 3.2 %collective-permute-done.6 = f32[128,160]{0,1:T(8,128)S(1)} collective-permute-done((f32[128,160]{0,1:T(8,128)S(1)}, f32[128,160]{0,1:T(8,128)S(1)}, u32[]{:S(2)}, u32[]{:S(2)}) %collective-permute-start.6) | collective-permute-done | bytes 81952 | tf_op jit(solution)/shard_map/ppermute | solution.py:99
  129.1 5.6 %collective-permute-done.7 = f32[128,160]{0,1:T(8,128)S(1)} collective-permute-done((f32[128,160]{0,1:T(8,128)S(1)}, f32[128,160]{0,1:T(8,128)S(1)}, u32[]{:S(2)}, u32[]{:S(2)}) %collective-permute-start.7) | collective-permute-done | bytes 81952 | tf_op jit(solution)/shard_map/ppermute | solution.py:99
  134.8 5.9 %collective-permute-done.8 = f32[128,160]{0,1:T(8,128)S(1)} collective-permute-done((f32[128,160]{0,1:T(8,128)S(1)}, f32[128,160]{0,1:T(8,128)S(1)}, u32[]{:S(2)}, u32[]{:S(2)}) %collective-permute-start.8) | collective-permute-done | bytes 81952 | tf_op jit(solution)/shard_map/ppermute | solution.py:99
  140.9 4.5 %collective-permute-done.9 = f32[128,160]{0,1:T(8,128)S(1)} collective-permute-done((f32[128,160]{0,1:T(8,128)S(1)}, f32[128,160]{0,1:T(8,128)S(1)}, u32[]{:S(2)}, u32[]{:S(2)}) %collective-permute-start.9) | collective-permute-done | bytes 81952 | tf_op jit(solution)/shard_map/ppermute | solution.py:99
  145.5 6.4 %collective-permute-done.10 = f32[128,160]{0,1:T(8,128)S(1)} collective-permute-done((f32[128,160]{0,1:T(8,128)S(1)}, f32[128,160]{0,1:T(8,128)S(1)}, u32[]{:S(2)}, u32[]{:S(2)}) %collective-permute-start.10) | collective-permute-done | bytes 81952 | tf_op jit(solution)/shard_map/ppermute | solution.py:99
  151.9 3.0 %collective-permute-start.11 = (f32[128,160]{0,1:T(8,128)S(1)}, f32[128,160]{0,1:T(8,128)S(1)}, u32[]{:S(2)}, u32[]{:S(2)}) collective-permute-start(f32[128,160]{0,1:T(8,128)S(1)} %add.167), channel_id=1, source_target_pairs={{0,128},{16,144},{32,160},{48,176},{64,192},{80,208},{96,224},{112... | collective-permute-start | bytes 245768 | tf_op jit(solution)/shard_map/ppermute | solution.py:99
  154.8 5.8 %collective-permute-done.11 = f32[128,160]{0,1:T(8,128)S(1)} collective-permute-done((f32[128,160]{0,1:T(8,128)S(1)}, f32[128,160]{0,1:T(8,128)S(1)}, u32[]{:S(2)}, u32[]{:S(2)}) %collective-permute-start.11) | collective-permute-done | bytes 81952 | tf_op jit(solution)/shard_map/ppermute | solution.py:99
  161.0 4.4 %collective-permute-done.12 = f32[128,160]{0,1:T(8,128)S(1)} collective-permute-done((f32[128,160]{0,1:T(8,128)S(1)}, f32[128,160]{0,1:T(8,128)S(1)}, u32[]{:S(2)}, u32[]{:S(2)}) %collective-permute-start.12) | collective-permute-done | bytes 81952 | tf_op jit(solution)/shard_map/ppermute | solution.py:99
  165.6 11.7 %cholesky.44 = f32[128,128]{1,0:T(8,128)S(1)} custom-call(f32[128,128]{1,0:T(8,128)S(1)} %fusion.38), custom_call_target="Cholesky" | custom-call | tf_op jit(solution)/shard_map/jit(cholesky)/cholesky | solution.py:68
  178.6 9.8 %custom-call.10 = f32[1,128,128]{1,2,0:T(8,128)S(1)} custom-call(f32[1,128,128]{2,1,0:T(8,128)S(1)} %fusion.27), custom_call_target="InvertDiagBlocksLowerTriangular" | custom-call | tf_op jit(solution)/shard_map/triangular_solve | solution.py:69
  191.5 11.7 %cholesky.55 = f32[128,128]{1,0:T(8,128)S(1)} custom-call(f32[128,128]{1,0:T(8,128)S(1)} %fusion.34), custom_call_target="Cholesky" | custom-call | tf_op jit(solution)/shard_map/jit(cholesky)/cholesky | solution.py:78
  204.6 9.8 %custom-call.11 = f32[1,128,128]{1,2,0:T(8,128)S(1)} custom-call(f32[1,128,128]{2,1,0:T(8,128)S(1)} %fusion.28), custom_call_target="InvertDiagBlocksLowerTriangular" | custom-call | tf_op jit(solution)/shard_map/triangular_solve | solution.py:80
  (187 shorter events, 45.1 us)
Async XLA Ops:
  0.6 10.6 %copy-start.3 = (s32[1,8,256]{2,1,0:T(8,128)S(1)}, s32[1,8,256]{2,1,0:T(8,128)}, u32[]{:S(2)}) copy-start(s32[1,8,256]{2,1,0:T(8,128)} %param.12) | copy-start | bytes 24580
  0.7 10.7 %copy-start.4 = (f32[1,4096]{1,0:T(1,128)S(1)}, f32[1,4096]{1,0:T(1,128)}, u32[]{:S(2)}) copy-start(f32[1,4096]{1,0:T(1,128)} %param.11) | copy-start | bytes 49156
  1.6 10.4 %collective-permute-start.3 = (f32[16,1024]{1,0:T(8,128)S(1)}, f32[16,1024]{1,0:T(8,128)S(1)}, u32[]{:S(2)}, u32[]{:S(2)}) collective-permute-start(f32[16,1024]{1,0:T(8,128)S(1)} %bitcast.323), channel_id=1, source_target_pairs={{1,16},{17,32},{33,48},{49,64},{65,80},{81,96},{97,112},{113,128},... | collective-permute-start | bytes 196616 | tf_op jit(solution)/shard_map/ppermute | solution.py:133
  10.8 24.7 %collective-permute-start.4 = (f32[16,3072]{1,0:T(8,128)S(1)}, f32[16,3072]{1,0:T(8,128)S(1)}, u32[]{:S(2)}, u32[]{:S(2)}) collective-permute-start(f32[16,3072]{1,0:T(8,128)S(1)} %bitcast.321), channel_id=1, source_target_pairs={{0,1},{1,0},{2,3},{3,2},{4,5},{5,4},{6,7},{7,6},{8,9},{9,8},{10,11... | collective-permute-start | bytes 589832 | tf_op jit(solution)/shard_map/ppermute | solution.py:28
  11.0 8.3 %collective-permute-start.2 = (f32[19,1024]{1,0:T(8,128)S(1)}, f32[19,1024]{1,0:T(8,128)S(1)}, u32[]{:S(2)}, u32[]{:S(2)}) collective-permute-start(f32[19,1024]{1,0:T(8,128)S(1)} %pad_maximum_fusion.8), channel_id=1, source_target_pairs={{0,16},{16,32},{32,48},{48,64},{64,80},{80,96},{96,112},{112,128},... | collective-permute-start | bytes 233480 | tf_op jit(solution)/shard_map/ppermute | solution.py:132
  35.5 12.2 %copy-start.1 = (f32[8,9,256,256]{3,2,1,0:T(8,128)}, f32[8,9,256,256]{3,2,1,0:T(8,128)S(1)}, u32[]{:S(2)}) copy-start(f32[8,9,256,256]{3,2,1,0:T(8,128)S(1)} %multiply_multiply_fusion) | copy-start | bytes 56623108
  48.1 5.0 %collective-permute-start = (f32[32,1024]{1,0:T(8,128)S(1)}, f32[32,1024]{1,0:T(8,128)S(1)}, u32[]{:S(2)}, u32[]{:S(2)}) collective-permute-start(f32[32,1024]{1,0:T(8,128)S(1)} %get-tuple-element.250), channel_id=1, source_target_pairs={{1,0},{16,1},{17,16},{32,17},{33,32},{48,33},{49,48},{64,49},{65,6... | collective-permute-start | bytes 393224 | tf_op jit(solution)/shard_map/while/body/eval_jaxpr/ppermute | solution.py:23
  49.6 8.3 %collective-permute-start.1 = (f32[32,1024]{1,0:T(8,128)S(1)}, f32[32,1024]{1,0:T(8,128)S(1)}, u32[]{:S(2)}, u32[]{:S(2)}) collective-permute-start(f32[32,1024]{1,0:T(8,128)S(1)} %get-tuple-element.251), channel_id=1, source_target_pairs={{0,1},{1,16},{16,17},{17,32},{32,33},{33,48},{48,49},{49,64},{64,6... | collective-permute-start | bytes 393224 | tf_op jit(solution)/shard_map/while/body/eval_jaxpr/ppermute | solution.py:22
  73.2 5.0 %collective-permute-start = (f32[32,1024]{1,0:T(8,128)S(1)}, f32[32,1024]{1,0:T(8,128)S(1)}, u32[]{:S(2)}, u32[]{:S(2)}) collective-permute-start(f32[32,1024]{1,0:T(8,128)S(1)} %get-tuple-element.250), channel_id=1, source_target_pairs={{1,0},{16,1},{17,16},{32,17},{33,32},{48,33},{49,48},{64,49},{65,6... | collective-permute-start | bytes 393224 | tf_op jit(solution)/shard_map/while/body/eval_jaxpr/ppermute | solution.py:23
  73.2 8.4 %collective-permute-start.1 = (f32[32,1024]{1,0:T(8,128)S(1)}, f32[32,1024]{1,0:T(8,128)S(1)}, u32[]{:S(2)}, u32[]{:S(2)}) collective-permute-start(f32[32,1024]{1,0:T(8,128)S(1)} %get-tuple-element.251), channel_id=1, source_target_pairs={{0,1},{1,16},{16,17},{17,32},{32,33},{33,48},{48,49},{49,64},{64,6... | collective-permute-start | bytes 393224 | tf_op jit(solution)/shard_map/while/body/eval_jaxpr/ppermute | solution.py:22
  96.9 5.0 %collective-permute-start = (f32[32,1024]{1,0:T(8,128)S(1)}, f32[32,1024]{1,0:T(8,128)S(1)}, u32[]{:S(2)}, u32[]{:S(2)}) collective-permute-start(f32[32,1024]{1,0:T(8,128)S(1)} %get-tuple-element.250), channel_id=1, source_target_pairs={{1,0},{16,1},{17,16},{32,17},{33,32},{48,33},{49,48},{64,49},{65,6... | collective-permute-start | bytes 393224 | tf_op jit(solution)/shard_map/while/body/eval_jaxpr/ppermute | solution.py:23
  97.0 8.4 %collective-permute-start.1 = (f32[32,1024]{1,0:T(8,128)S(1)}, f32[32,1024]{1,0:T(8,128)S(1)}, u32[]{:S(2)}, u32[]{:S(2)}) collective-permute-start(f32[32,1024]{1,0:T(8,128)S(1)} %get-tuple-element.251), channel_id=1, source_target_pairs={{0,1},{1,16},{16,17},{17,32},{32,33},{33,48},{48,49},{49,64},{64,6... | collective-permute-start | bytes 393224 | tf_op jit(solution)/shard_map/while/body/eval_jaxpr/ppermute | solution.py:22
  122.7 1.4 collective-permute-start.5
  124.1 4.6 %collective-permute-start.6 = (f32[128,160]{0,1:T(8,128)S(1)}, f32[128,160]{0,1:T(8,128)S(1)}, u32[]{:S(2)}, u32[]{:S(2)}) collective-permute-start(f32[128,160]{0,1:T(8,128)S(1)} %add.162), channel_id=1, source_target_pairs={{0,4},{2,6},{4,0},{6,2},{8,12},{10,14},{12,8},{14,10},{1,5},{3,7},... | collective-permute-start | bytes 245768 | tf_op jit(solution)/shard_map/ppermute | solution.py:99
  128.7 6.0 %collective-permute-start.7 = (f32[128,160]{0,1:T(8,128)S(1)}, f32[128,160]{0,1:T(8,128)S(1)}, u32[]{:S(2)}, u32[]{:S(2)}) collective-permute-start(f32[128,160]{0,1:T(8,128)S(1)} %add.163), channel_id=1, source_target_pairs={{0,8},{2,10},{4,12},{6,14},{8,0},{10,2},{12,4},{14,6},{1,9},{3,11}... | collective-permute-start | bytes 245768 | tf_op jit(solution)/shard_map/ppermute | solution.py:99
  134.7 6.0 %collective-permute-start.8 = (f32[128,160]{0,1:T(8,128)S(1)}, f32[128,160]{0,1:T(8,128)S(1)}, u32[]{:S(2)}, u32[]{:S(2)}) collective-permute-start(f32[128,160]{0,1:T(8,128)S(1)} %add.164), channel_id=1, source_target_pairs={{0,16},{16,0},{32,48},{48,32},{64,80},{80,64},{96,112},{112,96},{1... | collective-permute-start | bytes 245768 | tf_op jit(solution)/shard_map/ppermute | solution.py:99
  140.8 4.6 %collective-permute-start.9 = (f32[128,160]{0,1:T(8,128)S(1)}, f32[128,160]{0,1:T(8,128)S(1)}, u32[]{:S(2)}, u32[]{:S(2)}) collective-permute-start(f32[128,160]{0,1:T(8,128)S(1)} %add.165), channel_id=1, source_target_pairs={{0,32},{16,48},{32,0},{48,16},{64,96},{80,112},{96,64},{112,80},{1... | collective-permute-start | bytes 245768 | tf_op jit(solution)/shard_map/ppermute | solution.py:99
  145.4 6.5 %collective-permute-start.10 = (f32[128,160]{0,1:T(8,128)S(1)}, f32[128,160]{0,1:T(8,128)S(1)}, u32[]{:S(2)}, u32[]{:S(2)}) collective-permute-start(f32[128,160]{0,1:T(8,128)S(1)} %add.166), channel_id=1, source_target_pairs={{0,64},{16,80},{32,96},{48,112},{64,0},{80,16},{96,32},{112,48},{1... | collective-permute-start | bytes 245768 | tf_op jit(solution)/shard_map/ppermute | solution.py:99
  151.9 8.8 %collective-permute-start.11 = (f32[128,160]{0,1:T(8,128)S(1)}, f32[128,160]{0,1:T(8,128)S(1)}, u32[]{:S(2)}, u32[]{:S(2)}) collective-permute-start(f32[128,160]{0,1:T(8,128)S(1)} %add.167), channel_id=1, source_target_pairs={{0,128},{16,144},{32,160},{48,176},{64,192},{80,208},{96,224},{112... | collective-permute-start | bytes 245768 | tf_op jit(solution)/shard_map/ppermute | solution.py:99
  160.7 4.7 %collective-permute-start.12 = (f32[128,160]{0,1:T(8,128)S(1)}, f32[128,160]{0,1:T(8,128)S(1)}, u32[]{:S(2)}, u32[]{:S(2)}) collective-permute-start(f32[128,160]{0,1:T(8,128)S(1)} %add.168), channel_id=1, source_target_pairs={{0,1},{1,0},{2,3},{3,2},{4,5},{5,4},{6,7},{7,6},{8,9},{9,8},{10,11... | collective-permute-start | bytes 245768 | tf_op jit(solution)/shard_map/ppermute | solution.py:99
  190.3 25.5 %copy-start.2 = (f32[32,2048]{1,0:T(8,128)S(1)}, f32[32,2048]{1,0:T(8,128)}, u32[]{:S(2)}) copy-start(f32[32,2048]{1,0:T(8,128)} %get-tuple-element.176) | copy-start | bytes 786436
  190.3 34.8 %collective-permute-start.15 = (f32[64,2048]{1,0:T(8,128)S(1)}, f32[64,2048]{1,0:T(8,128)S(1)}, u32[]{:S(2)}, u32[]{:S(2)}) collective-permute-start(f32[64,2048]{1,0:T(8,128)S(1)} %get-tuple-element.175), channel_id=1, source_target_pairs={{0,1},{1,0},{2,3},{3,2},{4,5},{5,4},{6,7},{7,6},{8,9},{9,8},{10,11... | collective-permute-start | bytes 1572872 | tf_op jit(solution)/shard_map/ppermute | solution.py:28
  216.6 5.1 %collective-permute-start.14 = (f32[16,2048]{1,0:T(8,128)S(1)}, f32[16,2048]{1,0:T(8,128)S(1)}, u32[]{:S(2)}, u32[]{:S(2)}) collective-permute-start(f32[16,2048]{1,0:T(8,128)S(1)} %get-tuple-element.181), channel_id=1, source_target_pairs={{0,1},{1,0},{2,3},{3,2},{4,5},{5,4},{6,7},{7,6},{8,9},{9,8},{10,11... | collective-permute-start | bytes 393224 | tf_op jit(solution)/shard_map/ppermute | solution.py:28
  218.8 5.1 %collective-permute-start.13 = (f32[16,2048]{1,0:T(8,128)S(1)}, f32[16,2048]{1,0:T(8,128)S(1)}, u32[]{:S(2)}, u32[]{:S(2)}) collective-permute-start(f32[16,2048]{1,0:T(8,128)S(1)} %get-tuple-element.183), channel_id=1, source_target_pairs={{0,1},{1,0},{2,3},{3,2},{4,5},{5,4},{6,7},{7,6},{8,9},{9,8},{10,11... | collective-permute-start | bytes 393224 | tf_op jit(solution)/shard_map/ppermute | solution.py:28
  (1 other events, 10.3 us)

commit v2 on v0

--- a/solution.py
+++ b/solution.py
@@ -178,12 +178,18 @@
     correction = jnp.dot(combo, first_rows, precision=exact)
     new_residual = field - jnp.dot(combo, image, precision=exact)
     basis = jnp.dot(inverse_low, first_rows, precision=exact)
-    results = []
+    kept, given = [], []
     for full in (correction, new_residual, basis):
         groups = full.reshape(pairs, -1, half)
-        keep = lax.dynamic_index_in_dim(groups, part, 0, False)
-        give = lax.dynamic_index_in_dim(groups, 1 - part, 0, False)
-        results.append(in_order(keep, swap_pair(give, part), part, 1)[:, None])
+        kept.append(lax.dynamic_index_in_dim(groups, part, 0, False))
+        given.append(lax.dynamic_index_in_dim(groups, 1 - part, 0, False))
+    got = swap_pair(jnp.concatenate(given, axis=0), part)
+    joined = in_order(jnp.concatenate(kept, axis=0), got, part, 1)
+    results = []
+    start = 0
+    for piece in kept:
+        results.append(joined[start : start + piece.shape[0], None])
+        start += piece.shape[0]
     return tuple(results)
 
 

time: 228 us -> 229 us (level)
  waiting for transfers between devices: 58.6 us -> 64 us
  other arithmetic: 71.2 us -> 66.6 us
  local copies, waits for them, and re-layouts: 7.58 us -> 10.7 us
    ppermute x4 -> x2, waiting for transfers between devices: 6.66 us -> 12 us  [swap_pair(): return lax.ppermute(x, 'rhs', [(0, 1), (1, 0)])]
    select_n x3 -> x1, other arithmetic: 4.87 us -> 0.16 us  [in_order(): return jnp.where(part == 0, first, second)]
    broadcast_in_dim x0 -> x3, local copies, waits for them, and re-layouts: none -> 4.09 us  [local(): results.append(joined[start:start + piece.shape[0], None])]
  transfers between devices with their start and end apart: 20 -> 18, of which waited for: 15 -> 13; matrix products, arithmetic and copies ran while one was open for 10% -> 8% of each run, Pallas kernels for 0% -> 0%
where the time goes in v2:
time: 229 us; the launch traced here: 225 us
  other arithmetic  66.6 us (29%)
  waiting for transfers between devices  64 us (28%)
  matrix products  51.6 us (23%)
  starting transfers between devices  30.6 us (13%)
  local copies, waits for them, and re-layouts  10.7 us (5%)
    dot_general x4, matrix products, band_product(): out = jnp.einsum('mbkq,bkqp->mbp', near, tiles, precision=exact)  46.1 us
    ppermute x8, waiting for transfers between devices, butterfly_sum(): x = x + lax.ppermute(x, axis, [(i, i ^ step) for i in range(count)])  39.4 us
    ppermute x3, starting transfers between devices, extended(): after = lax.ppermute(x[:, :width], axes, down)  17.1 us
    mul x2, other arithmetic, band_tiles(): return tiles * jnp.transpose(weights)[:, :, None, None]  15.6 us
    another operation x3, other arithmetic, galerkin(): factor_low = jnp.linalg.cholesky(gram_basis)  12.4 us
    another operation x3, other arithmetic, galerkin(): proj_factor = jnp.linalg.cholesky(projected)  12.4 us
    ppermute x2, waiting for transfers between devices, swap_pair(): return lax.ppermute(x, 'rhs', [(0, 1), (1, 0)])  12 us
    another operation x2, other arithmetic, galerkin(): lax.linalg.triangular_solve(proj_factor, halfway, left_side=True, lower=T...  10.7 us
  transfers between devices with their start and end apart: 18, of which 13 were waited for; matrix products, arithmetic and copies ran while one was open for 8% of the time, Pallas kernels for 0%

profile of v2, /device:TPU:16, one launch (start us, length us, event | category | flops | bytes accessed | tf_op | source)
XLA Modules:
  0.0 225.4 jit_solution(3914101150003298133)
XLA Ops:
  1.6 8.1 %collective-permute-start.1 = (f32[16,1024]{1,0:T(8,128)S(1)}, f32[16,1024]{1,0:T(8,128)S(1)}, u32[]{:S(2)}, u32[]{:S(2)}) collective-permute-start(f32[16,1024]{1,0:T(8,128)S(1)} %bitcast.380), channel_id=1, source_target_pairs={{1,16},{17,32},{33,48},{49,64},{65,80},{81,96},{97,112},{113,128},... | collective-permute-start | bytes 196616 | tf_op jit(solution)/shard_map/ppermute | solution.py:133
  13.7 4.4 %collective-permute-done = f32[19,1024]{1,0:T(8,128)S(1)} collective-permute-done((f32[19,1024]{1,0:T(8,128)S(1)}, f32[19,1024]{1,0:T(8,128)S(1)}, u32[]{:S(2)}, u32[]{:S(2)}) %collective-permute-start) | collective-permute-done | bytes 77856 | tf_op jit(solution)/shard_map/ppermute | solution.py:132
  18.4 15.5 %multiply_multiply_fusion = f32[8,9,256,256]{3,2,1,0:T(8,128)S(1)} fusion(f32[8,9]{1,0:T(8,128)S(1)} %copy.49, f32[8,256]{1,0:T(8,128)S(1)} %get-tuple-element.67, f32[8,9,256]{2,1,0:T(8,128)S(1)} %copy.48, f32[8,256]{1,0:T(8,128)S(1)} %get-tuple-element.68, f32[8,9,256]{2,1,0:T(8,128)S(1)} %copy.47, f32[8,256]{1,0:T(8,128)S(1)} %get-tuple-element.66, ...), kind=kLoop, calls=%fused_computation | loop fusion | flops 80216064 | bytes 19120416 | tf_op jit(solution)/shard_map/mul | solution.py:52
  35.2 11.5 %convolution_bitcast_fusion.3 = f32[8,4,8,256]{3,2,1,0:T(8,128)S(1)} fusion(f32[8,9,256,256]{3,2,1,0:T(8,128)S(1)} %multiply_multiply_fusion, f32[32,8,9,256]{3,0,2,1:T(8,128)S(1)} %fusion.8), kind=kOutput, calls=%fused_computation.6 | convolution fusion | flops 1811939328 | bytes 21495808 | tf_op jit(solution)/shard_map/mbkq,bkqp->mbp/dot_general | solution.py:60
  47.6 5.8 %collective-permute-start.4 = (f32[32,1024]{1,0:T(8,128)S(1)}, f32[32,1024]{1,0:T(8,128)S(1)}, u32[]{:S(2)}, u32[]{:S(2)}) collective-permute-start(f32[32,1024]{1,0:T(8,128)S(1)} %get-tuple-element.54), channel_id=1, source_target_pairs={{1,0},{16,1},{17,16},{32,17},{33,32},{48,33},{49,48},{64,49},{65,6... | collective-permute-start | bytes 393224 | tf_op jit(solution)/shard_map/ppermute | solution.py:23
  57.1 11.5 %convolution_bitcast_fusion.2 = f32[8,4,8,256]{3,2,1,0:T(8,128)S(1)} fusion(f32[8,9,256,256]{3,2,1,0:T(8,128)S(1)} %multiply_multiply_fusion, f32[32,8,9,256]{3,0,2,1:T(8,128)S(1)} %fusion.36), kind=kOutput, calls=%fused_computation.5 | convolution fusion | flops 1811939328 | bytes 21495808 | tf_op jit(solution)/shard_map/mbkq,bkqp->mbp/dot_general | solution.py:60
  69.7 5.8 %collective-permute-start.6 = (f32[32,1024]{1,0:T(8,128)S(1)}, f32[32,1024]{1,0:T(8,128)S(1)}, u32[]{:S(2)}, u32[]{:S(2)}) collective-permute-start(f32[32,1024]{1,0:T(8,128)S(1)} %get-tuple-element.52), channel_id=1, source_target_pairs={{1,0},{16,1},{17,16},{32,17},{33,32},{48,33},{49,48},{64,49},{65,6... | collective-permute-start | bytes 393224 | tf_op jit(solution)/shard_map/ppermute | solution.py:23
  75.5 2.9 %collective-permute-done.5 = f32[32,1024]{1,0:T(8,128)S(1)} collective-permute-done((f32[32,1024]{1,0:T(8,128)S(1)}, f32[32,1024]{1,0:T(8,128)S(1)}, u32[]{:S(2)}, u32[]{:S(2)}) %collective-permute-start.5) | collective-permute-done | bytes 131104 | tf_op jit(solution)/shard_map/ppermute | solution.py:22
  79.6 11.5 %convolution_bitcast_fusion.1 = f32[8,4,8,256]{3,2,1,0:T(8,128)S(1)} fusion(f32[8,9,256,256]{3,2,1,0:T(8,128)S(1)} %multiply_multiply_fusion, f32[32,8,9,256]{3,0,2,1:T(8,128)S(1)} %fusion.27), kind=kOutput, calls=%fused_computation.4 | convolution fusion | flops 1811939328 | bytes 21495808 | tf_op jit(solution)/shard_map/mbkq,bkqp->mbp/dot_general | solution.py:60
  92.4 5.5 %collective-permute-start.8 = (f32[32,1024]{1,0:T(8,128)S(1)}, f32[32,1024]{1,0:T(8,128)S(1)}, u32[]{:S(2)}, u32[]{:S(2)}) collective-permute-start(f32[32,1024]{1,0:T(8,128)S(1)} %get-tuple-element.50), channel_id=1, source_target_pairs={{1,0},{16,1},{17,16},{32,17},{33,32},{48,33},{49,48},{64,49},{65,6... | collective-permute-start | bytes 393224 | tf_op jit(solution)/shard_map/ppermute | solution.py:23
  97.9 2.9 %collective-permute-done.7 = f32[32,1024]{1,0:T(8,128)S(1)} collective-permute-done((f32[32,1024]{1,0:T(8,128)S(1)}, f32[32,1024]{1,0:T(8,128)S(1)}, u32[]{:S(2)}, u32[]{:S(2)}) %collective-permute-start.7) | collective-permute-done | bytes 131104 | tf_op jit(solution)/shard_map/ppermute | solution.py:22
  102.0 11.5 %convolution_bitcast_fusion = f32[8,4,8,256]{3,2,1,0:T(8,128)S(1)} fusion(f32[8,9,256,256]{3,2,1,0:T(8,128)S(1)} %multiply_multiply_fusion, f32[32,8,9,256]{3,0,2,1:T(8,128)S(1)} %fusion.18), kind=kOutput, calls=%fused_computation.3 | convolution fusion | flops 1811939328 | bytes 21495808 | tf_op jit(solution)/shard_map/mbkq,bkqp->mbp/dot_general | solution.py:60
  117.8 3.2 %collective-permute-done.10 = f32[128,160]{0,1:T(8,128)S(1)} collective-permute-done((f32[128,160]{0,1:T(8,128)S(1)}, f32[128,160]{0,1:T(8,128)S(1)}, u32[]{:S(2)}, u32[]{:S(2)}) %collective-permute-start.10) | collective-permute-done | bytes 81952 | tf_op jit(solution)/shard_map/ppermute | solution.py:99
  121.4 5.6 %collective-permute-done.11 = f32[128,160]{0,1:T(8,128)S(1)} collective-permute-done((f32[128,160]{0,1:T(8,128)S(1)}, f32[128,160]{0,1:T(8,128)S(1)}, u32[]{:S(2)}, u32[]{:S(2)}) %collective-permute-start.11) | collective-permute-done | bytes 81952 | tf_op jit(solution)/shard_map/ppermute | solution.py:99
  127.2 5.9 %collective-permute-done.12 = f32[128,160]{0,1:T(8,128)S(1)} collective-permute-done((f32[128,160]{0,1:T(8,128)S(1)}, f32[128,160]{0,1:T(8,128)S(1)}, u32[]{:S(2)}, u32[]{:S(2)}) %collective-permute-start.12) | collective-permute-done | bytes 81952 | tf_op jit(solution)/shard_map/ppermute | solution.py:99
  133.2 4.5 %collective-permute-done.13 = f32[128,160]{0,1:T(8,128)S(1)} collective-permute-done((f32[128,160]{0,1:T(8,128)S(1)}, f32[128,160]{0,1:T(8,128)S(1)}, u32[]{:S(2)}, u32[]{:S(2)}) %collective-permute-start.13) | collective-permute-done | bytes 81952 | tf_op jit(solution)/shard_map/ppermute | solution.py:99
  137.8 7.1 %collective-permute-done.14 = f32[128,160]{0,1:T(8,128)S(1)} collective-permute-done((f32[128,160]{0,1:T(8,128)S(1)}, f32[128,160]{0,1:T(8,128)S(1)}, u32[]{:S(2)}, u32[]{:S(2)}) %collective-permute-start.14) | collective-permute-done | bytes 81952 | tf_op jit(solution)/shard_map/ppermute | solution.py:99
  146.1 7.3 %collective-permute-done.15 = f32[128,160]{0,1:T(8,128)S(1)} collective-permute-done((f32[128,160]{0,1:T(8,128)S(1)}, f32[128,160]{0,1:T(8,128)S(1)}, u32[]{:S(2)}, u32[]{:S(2)}) %collective-permute-start.15) | collective-permute-done | bytes 81952 | tf_op jit(solution)/shard_map/ppermute | solution.py:99
  153.5 4.4 %collective-permute-done.16 = f32[128,160]{0,1:T(8,128)S(1)} collective-permute-done((f32[128,160]{0,1:T(8,128)S(1)}, f32[128,160]{0,1:T(8,128)S(1)}, u32[]{:S(2)}, u32[]{:S(2)}) %collective-permute-start.16) | collective-permute-done | bytes 81952 | tf_op jit(solution)/shard_map/ppermute | solution.py:99
  158.1 11.7 %cholesky.44 = f32[128,128]{1,0:T(8,128)S(1)} custom-call(f32[128,128]{1,0:T(8,128)S(1)} %fusion.56), custom_call_target="Cholesky" | custom-call | tf_op jit(solution)/shard_map/jit(cholesky)/cholesky | solution.py:68
  171.2 9.8 %custom-call.10 = f32[1,128,128]{1,2,0:T(8,128)S(1)} custom-call(f32[1,128,128]{2,1,0:T(8,128)S(1)} %fusion.45), custom_call_target="InvertDiagBlocksLowerTriangular" | custom-call | tf_op jit(solution)/shard_map/triangular_solve | solution.py:69
  183.2 11.7 %cholesky.55 = f32[128,128]{1,0:T(8,128)S(1)} custom-call(f32[128,128]{1,0:T(8,128)S(1)} %fusion.52), custom_call_target="Cholesky" | custom-call | tf_op jit(solution)/shard_map/jit(cholesky)/cholesky | solution.py:78
  196.3 10.0 %custom-call.11 = f32[1,128,128]{1,2,0:T(8,128)S(1)} custom-call(f32[1,128,128]{2,1,0:T(8,128)S(1)} %fusion.46), custom_call_target="InvertDiagBlocksLowerTriangular" | custom-call | tf_op jit(solution)/shard_map/triangular_solve | solution.py:80
  208.8 12.0 %collective-permute-done.17 = f32[96,2048]{1,0:T(8,128)S(1)} collective-permute-done((f32[96,2048]{1,0:T(8,128)S(1)}, f32[96,2048]{1,0:T(8,128)S(1)}, u32[]{:S(2)}, u32[]{:S(2)}) %collective-permute-start.17) | collective-permute-done | bytes 786464 | tf_op jit(solution)/shard_map/ppermute | solution.py:28
  (168 shorter events, 33.2 us)
Async XLA Ops:
  0.6 9.1 %copy-start = (f32[3,1,4096]{2,1,0:T(1,128)S(1)}, f32[3,1,4096]{2,1,0:T(1,128)}, u32[]{:S(2)}) copy-start(f32[3,1,4096]{2,1,0:T(1,128)} %param.6) | copy-start | bytes 147460
  1.6 12.1 %collective-permute-start.1 = (f32[16,1024]{1,0:T(8,128)S(1)}, f32[16,1024]{1,0:T(8,128)S(1)}, u32[]{:S(2)}, u32[]{:S(2)}) collective-permute-start(f32[16,1024]{1,0:T(8,128)S(1)} %bitcast.380), channel_id=1, source_target_pairs={{1,16},{17,32},{33,48},{49,64},{65,80},{81,96},{97,112},{113,128},... | collective-permute-start | bytes 196616 | tf_op jit(solution)/shard_map/ppermute | solution.py:133
  9.8 8.3 %collective-permute-start = (f32[19,1024]{1,0:T(8,128)S(1)}, f32[19,1024]{1,0:T(8,128)S(1)}, u32[]{:S(2)}, u32[]{:S(2)}) collective-permute-start(f32[19,1024]{1,0:T(8,128)S(1)} %pad_maximum_fusion.11), channel_id=1, source_target_pairs={{0,16},{16,32},{32,48},{48,64},{64,80},{80,96},{96,112},{112,128},... | collective-permute-start | bytes 233480 | tf_op jit(solution)/shard_map/ppermute | solution.py:132
  11.0 23.0 %collective-permute-start.2 = (f32[16,3072]{1,0:T(8,128)S(1)}, f32[16,3072]{1,0:T(8,128)S(1)}, u32[]{:S(2)}, u32[]{:S(2)}) collective-permute-start(f32[16,3072]{1,0:T(8,128)S(1)} %bitcast.378), channel_id=1, source_target_pairs={{0,1},{1,0},{2,3},{3,2},{4,5},{5,4},{6,7},{7,6},{8,9},{9,8},{10,11... | collective-permute-start | bytes 589832 | tf_op jit(solution)/shard_map/ppermute | solution.py:28
  47.5 8.4 %collective-permute-start.3 = (f32[32,1024]{1,0:T(8,128)S(1)}, f32[32,1024]{1,0:T(8,128)S(1)}, u32[]{:S(2)}, u32[]{:S(2)}) collective-permute-start(f32[32,1024]{1,0:T(8,128)S(1)} %get-tuple-element.53), channel_id=1, source_target_pairs={{0,1},{1,16},{16,17},{17,32},{32,33},{33,48},{48,49},{49,64},{64,6... | collective-permute-start | bytes 393224 | tf_op jit(solution)/shard_map/ppermute | solution.py:22
  47.6 8.3 %collective-permute-start.4 = (f32[32,1024]{1,0:T(8,128)S(1)}, f32[32,1024]{1,0:T(8,128)S(1)}, u32[]{:S(2)}, u32[]{:S(2)}) collective-permute-start(f32[32,1024]{1,0:T(8,128)S(1)} %get-tuple-element.54), channel_id=1, source_target_pairs={{1,0},{16,1},{17,16},{32,17},{33,32},{48,33},{49,48},{64,49},{65,6... | collective-permute-start | bytes 393224 | tf_op jit(solution)/shard_map/ppermute | solution.py:23
  69.4 9.0 %collective-permute-start.5 = (f32[32,1024]{1,0:T(8,128)S(1)}, f32[32,1024]{1,0:T(8,128)S(1)}, u32[]{:S(2)}, u32[]{:S(2)}) collective-permute-start(f32[32,1024]{1,0:T(8,128)S(1)} %get-tuple-element.51), channel_id=1, source_target_pairs={{0,1},{1,16},{16,17},{17,32},{32,33},{33,48},{48,49},{49,64},{64,6... | collective-permute-start | bytes 393224 | tf_op jit(solution)/shard_map/ppermute | solution.py:22
  69.7 8.7 %collective-permute-start.6 = (f32[32,1024]{1,0:T(8,128)S(1)}, f32[32,1024]{1,0:T(8,128)S(1)}, u32[]{:S(2)}, u32[]{:S(2)}) collective-permute-start(f32[32,1024]{1,0:T(8,128)S(1)} %get-tuple-element.52), channel_id=1, source_target_pairs={{1,0},{16,1},{17,16},{32,17},{33,32},{48,33},{49,48},{64,49},{65,6... | collective-permute-start | bytes 393224 | tf_op jit(solution)/shard_map/ppermute | solution.py:23
  91.9 8.9 %collective-permute-start.7 = (f32[32,1024]{1,0:T(8,128)S(1)}, f32[32,1024]{1,0:T(8,128)S(1)}, u32[]{:S(2)}, u32[]{:S(2)}) collective-permute-start(f32[32,1024]{1,0:T(8,128)S(1)} %get-tuple-element.49), channel_id=1, source_target_pairs={{0,1},{1,16},{16,17},{17,32},{32,33},{33,48},{48,49},{49,64},{64,6... | collective-permute-start | bytes 393224 | tf_op jit(solution)/shard_map/ppermute | solution.py:22
  92.4 8.4 %collective-permute-start.8 = (f32[32,1024]{1,0:T(8,128)S(1)}, f32[32,1024]{1,0:T(8,128)S(1)}, u32[]{:S(2)}, u32[]{:S(2)}) collective-permute-start(f32[32,1024]{1,0:T(8,128)S(1)} %get-tuple-element.50), channel_id=1, source_target_pairs={{1,0},{16,1},{17,16},{32,17},{33,32},{48,33},{49,48},{64,49},{65,6... | collective-permute-start | bytes 393224 | tf_op jit(solution)/shard_map/ppermute | solution.py:23
  102.0 11.6 %copy-start.1 = (f32[160,2048]{1,0:T(8,128)S(1)}, f32[160,2048]{1,0:T(8,128)}, u32[]{:S(2)}) copy-start(f32[160,2048]{1,0:T(8,128)} %get-tuple-element.6) | copy-start | bytes 3932164
  115.0 1.4 collective-permute-start.9
  116.4 4.6 %collective-permute-start.10 = (f32[128,160]{0,1:T(8,128)S(1)}, f32[128,160]{0,1:T(8,128)S(1)}, u32[]{:S(2)}, u32[]{:S(2)}) collective-permute-start(f32[128,160]{0,1:T(8,128)S(1)} %add.125), channel_id=1, source_target_pairs={{0,4},{2,6},{4,0},{6,2},{8,12},{10,14},{12,8},{14,10},{1,5},{3,7},... | collective-permute-start | bytes 245768 | tf_op jit(solution)/shard_map/ppermute | solution.py:99
  121.0 6.0 %collective-permute-start.11 = (f32[128,160]{0,1:T(8,128)S(1)}, f32[128,160]{0,1:T(8,128)S(1)}, u32[]{:S(2)}, u32[]{:S(2)}) collective-permute-start(f32[128,160]{0,1:T(8,128)S(1)} %add.126), channel_id=1, source_target_pairs={{0,8},{2,10},{4,12},{6,14},{8,0},{10,2},{12,4},{14,6},{1,9},{3,11}... | collective-permute-start | bytes 245768 | tf_op jit(solution)/shard_map/ppermute | solution.py:99
  127.1 6.0 %collective-permute-start.12 = (f32[128,160]{0,1:T(8,128)S(1)}, f32[128,160]{0,1:T(8,128)S(1)}, u32[]{:S(2)}, u32[]{:S(2)}) collective-permute-start(f32[128,160]{0,1:T(8,128)S(1)} %add.127), channel_id=1, source_target_pairs={{0,16},{16,0},{32,48},{48,32},{64,80},{80,64},{96,112},{112,96},{1... | collective-permute-start | bytes 245768 | tf_op jit(solution)/shard_map/ppermute | solution.py:99
  133.1 4.6 %collective-permute-start.13 = (f32[128,160]{0,1:T(8,128)S(1)}, f32[128,160]{0,1:T(8,128)S(1)}, u32[]{:S(2)}, u32[]{:S(2)}) collective-permute-start(f32[128,160]{0,1:T(8,128)S(1)} %add.128), channel_id=1, source_target_pairs={{0,32},{16,48},{32,0},{48,16},{64,96},{80,112},{96,64},{112,80},{1... | collective-permute-start | bytes 245768 | tf_op jit(solution)/shard_map/ppermute | solution.py:99
  137.7 7.2 %collective-permute-start.14 = (f32[128,160]{0,1:T(8,128)S(1)}, f32[128,160]{0,1:T(8,128)S(1)}, u32[]{:S(2)}, u32[]{:S(2)}) collective-permute-start(f32[128,160]{0,1:T(8,128)S(1)} %add.129), channel_id=1, source_target_pairs={{0,64},{16,80},{32,96},{48,112},{64,0},{80,16},{96,32},{112,48},{1... | collective-permute-start | bytes 245768 | tf_op jit(solution)/shard_map/ppermute | solution.py:99
  145.0 8.4 %collective-permute-start.15 = (f32[128,160]{0,1:T(8,128)S(1)}, f32[128,160]{0,1:T(8,128)S(1)}, u32[]{:S(2)}, u32[]{:S(2)}) collective-permute-start(f32[128,160]{0,1:T(8,128)S(1)} %add.130), channel_id=1, source_target_pairs={{0,128},{16,144},{32,160},{48,176},{64,192},{80,208},{96,224},{112... | collective-permute-start | bytes 245768 | tf_op jit(solution)/shard_map/ppermute | solution.py:99
  153.4 4.5 %collective-permute-start.16 = (f32[128,160]{0,1:T(8,128)S(1)}, f32[128,160]{0,1:T(8,128)S(1)}, u32[]{:S(2)}, u32[]{:S(2)}) collective-permute-start(f32[128,160]{0,1:T(8,128)S(1)} %add.131), channel_id=1, source_target_pairs={{0,1},{1,0},{2,3},{3,2},{4,5},{5,4},{6,7},{7,6},{8,9},{9,8},{10,11... | collective-permute-start | bytes 245768 | tf_op jit(solution)/shard_map/ppermute | solution.py:99
  208.7 12.1 %collective-permute-start.17 = (f32[96,2048]{1,0:T(8,128)S(1)}, f32[96,2048]{1,0:T(8,128)S(1)}, u32[]{:S(2)}, u32[]{:S(2)}) collective-permute-start(f32[96,2048]{1,0:T(8,128)S(1)} %pad_maximum_fusion.1), channel_id=1, source_target_pairs={{0,1},{1,0},{2,3},{3,2},{4,5},{5,4},{6,7},{7,6},{8,9},{9,8},{10,11... | collective-permute-start | bytes 2359304 | tf_op jit(solution)/shard_map/ppermute | solution.py:28

commit v3 on v0

--- a/solution.py
+++ b/solution.py
@@ -167,11 +167,15 @@
     current = field
     for power_step in range(S):
         widened = first_wide if power_step == 0 else extended(current, ("blk", "rhs"), ring, rim)
+        if power_step == S - 1:
+            basis_rows = jnp.concatenate(powers, axis=0)
+            gram_basis_part = row_products(basis_rows, basis_rows)
         current = band_product(widened, tiles, own_blocks) + (nugget - centre_shift) * current
         powers.append(current)
     flat = jnp.concatenate(powers, axis=0)
     count_points = half * ring * lax.axis_size("leaf")
-    gram = butterfly_sum(row_products(flat[: S * M], flat), ("leaf", "blk", "rhs"))
+    gram_part = jnp.concatenate([gram_basis_part, row_products(basis_rows, current)], axis=1)
+    gram = butterfly_sum(gram_part, ("leaf", "blk", "rhs"))
     inverse_low, combo = galerkin(gram, count_points, M)
     first_rows = flat[: S * M]
     image = flat[M:] + centre_shift * first_rows

time: 228 us -> 228 us (level)
  waiting for transfers between devices: 58.6 us -> 69.5 us
  starting transfers between devices: 32.8 us -> 23.9 us
  other arithmetic: 71.2 us -> 68.3 us
    ppermute x3, starting transfers between devices: 17.1 us -> 1.39 us  [extended(): after = lax.ppermute(x[:, :width], axes, down)]
    ppermute x1, starting transfers between devices: 8.14 us -> 0.65 us  [local(): lax.ppermute(lax.dynamic_slice_in_dim(own, part * inner, rim, 1), ring_ax...]
    ppermute x3, waiting for transfers between devices: 0.03 us -> 7.45 us  [extended(): after = lax.ppermute(x[:, :width], axes, down)]
    ppermute x1, waiting for transfers between devices: 0.01 us -> 5.27 us  [local(): lax.ppermute(lax.dynamic_slice_in_dim(own, part * inner, rim, 1), ring_ax...]
    ppermute x3, starting transfers between devices: 0.83 us -> 5.88 us  [extended(): before = lax.ppermute(x[:, length - width:], axes, up)]
    ppermute x4, starting transfers between devices: 3.24 us -> 8.26 us  [swap_pair(): return lax.ppermute(x, 'rhs', [(0, 1), (1, 0)])]
    ppermute x1, waiting for transfers between devices: 4.38 us -> 0.01 us  [local(): from_same = lax.ppermute(edge, ring_axes, same_side)]
    ppermute x1, starting transfers between devices: 0.08 us -> 3.1 us  [local(): from_same = lax.ppermute(edge, ring_axes, same_side)]
  transfers between devices with their start and end apart: 20 -> 20, of which waited for: 15 -> 18; matrix products, arithmetic and copies ran while one was open for 10% -> 10% of each run, Pallas kernels for 0% -> 0%
where the time goes in v3:
time: 228 us; the launch traced here: 224 us
  waiting for transfers between devices  69.5 us (30%)
  other arithmetic  68.3 us (30%)
  matrix products  52.5 us (23%)
  starting transfers between devices  23.9 us (10%)
  local copies, waits for them, and re-layouts  8.4 us (4%)
    dot_general x4, matrix products, band_product(): out = jnp.einsum('mbkq,bkqp->mbp', near, tiles, precision=exact)  46.3 us
    ppermute x8, waiting for transfers between devices, butterfly_sum(): x = x + lax.ppermute(x, axis, [(i, i ^ step) for i in range(count)])  39 us
    mul x2, other arithmetic, band_tiles(): return tiles * jnp.transpose(weights)[:, :, None, None]  15.6 us
    another operation x3, other arithmetic, galerkin(): proj_factor = jnp.linalg.cholesky(projected)  12.4 us
    another operation x3, other arithmetic, galerkin(): factor_low = jnp.linalg.cholesky(gram_basis)  12.4 us
    ppermute x3, waiting for transfers between devices, extended(): before = lax.ppermute(x[:, length - width:], axes, up)  11.1 us
    another operation x2, other arithmetic, galerkin(): lax.linalg.triangular_solve(proj_factor, halfway, left_side=True, lower=T...  10.6 us
    another operation x2, other arithmetic, galerkin(): lax.linalg.triangular_solve(factor_low, jnp.eye(basis_count, dtype=jnp.fl...  10.5 us
  transfers between devices with their start and end apart: 20, of which 18 were waited for; matrix products, arithmetic and copies ran while one was open for 10% of the time, Pallas kernels for 0%

profile of v3, /device:TPU:16, one launch (start us, length us, event | category | flops | bytes accessed | tf_op | source)
XLA Modules:
  0.0 224.4 jit_solution(5879921183209675170)
XLA Ops:
  2.4 3.1 %collective-permute-start = (f32[19,1024]{1,0:T(8,128)S(1)}, f32[19,1024]{1,0:T(8,128)S(1)}, u32[]{:S(2)}, u32[]{:S(2)}) collective-permute-start(f32[19,1024]{1,0:T(8,128)S(1)} %pad_maximum_fusion.10), channel_id=1, source_target_pairs={{0,16},{16,32},{32,48},{48,64},{64,80},{80,96},{96,112},{112,128},... | collective-permute-start | bytes 233480 | tf_op jit(solution)/shard_map/ppermute | solution.py:132
  6.6 6.0 %collective-permute-start.2 = (f32[16,3072]{1,0:T(8,128)S(1)}, f32[16,3072]{1,0:T(8,128)S(1)}, u32[]{:S(2)}, u32[]{:S(2)}) collective-permute-start(f32[16,3072]{1,0:T(8,128)S(1)} %bitcast.374), channel_id=1, source_target_pairs={{0,1},{1,0},{2,3},{3,2},{4,5},{5,4},{6,7},{7,6},{8,9},{9,8},{10,11... | collective-permute-start | bytes 589832 | tf_op jit(solution)/shard_map/ppermute | solution.py:28
  15.0 5.3 %collective-permute-done.1 = f32[16,1024]{1,0:T(8,128)S(1)} collective-permute-done((f32[16,1024]{1,0:T(8,128)S(1)}, f32[16,1024]{1,0:T(8,128)S(1)}, u32[]{:S(2)}, u32[]{:S(2)}) %collective-permute-start.1) | collective-permute-done | bytes 65568 | tf_op jit(solution)/shard_map/ppermute | solution.py:133
  20.6 15.5 %multiply_multiply_fusion = f32[8,9,256,256]{3,2,1,0:T(8,128)S(1)} fusion(f32[8,9]{1,0:T(8,128)S(1)} %copy.49, f32[8,256]{1,0:T(8,128)S(1)} %get-tuple-element.57, f32[8,9,256]{2,1,0:T(8,128)S(1)} %copy.48, f32[8,256]{1,0:T(8,128)S(1)} %get-tuple-element.58, f32[8,9,256]{2,1,0:T(8,128)S(1)} %copy.47, f32[8,256]{1,0:T(8,128)S(1)} %get-tuple-element.56, ...), kind=kLoop, calls=%fused_computation | loop fusion | flops 80216064 | bytes 19120416 | tf_op jit(solution)/shard_map/mul | solution.py:52
  36.7 11.5 %convolution_bitcast_fusion.3 = f32[8,4,8,256]{3,2,1,0:T(8,128)S(1)} fusion(f32[8,9,256,256]{3,2,1,0:T(8,128)S(1)} %multiply_multiply_fusion, f32[32,8,9,256]{3,0,2,1:T(8,128)S(1)} %fusion.8), kind=kOutput, calls=%fused_computation.6 | convolution fusion | flops 1811939328 | bytes 21495808 | tf_op jit(solution)/shard_map/mbkq,bkqp->mbp/dot_general | solution.py:60
  53.4 4.3 %collective-permute-done.3 = f32[32,1024]{1,0:T(8,128)S(1)} collective-permute-done((f32[32,1024]{1,0:T(8,128)S(1)}, f32[32,1024]{1,0:T(8,128)S(1)}, u32[]{:S(2)}, u32[]{:S(2)}) %collective-permute-start.3) | collective-permute-done | bytes 131104 | tf_op jit(solution)/shard_map/ppermute | solution.py:22
  58.9 11.5 %convolution_bitcast_fusion.2 = f32[8,4,8,256]{3,2,1,0:T(8,128)S(1)} fusion(f32[8,9,256,256]{3,2,1,0:T(8,128)S(1)} %multiply_multiply_fusion, f32[32,8,9,256]{3,0,2,1:T(8,128)S(1)} %fusion.36), kind=kOutput, calls=%fused_computation.5 | convolution fusion | flops 1811939328 | bytes 21495808 | tf_op jit(solution)/shard_map/mbkq,bkqp->mbp/dot_general | solution.py:60
  72.8 2.9 %collective-permute-done.6 = f32[32,1024]{1,0:T(8,128)S(1)} collective-permute-done((f32[32,1024]{1,0:T(8,128)S(1)}, f32[32,1024]{1,0:T(8,128)S(1)}, u32[]{:S(2)}, u32[]{:S(2)}) %collective-permute-start.6) | collective-permute-done | bytes 131104 | tf_op jit(solution)/shard_map/ppermute | solution.py:23
  75.7 3.4 %collective-permute-done.5 = f32[32,1024]{1,0:T(8,128)S(1)} collective-permute-done((f32[32,1024]{1,0:T(8,128)S(1)}, f32[32,1024]{1,0:T(8,128)S(1)}, u32[]{:S(2)}, u32[]{:S(2)}) %collective-permute-start.5) | collective-permute-done | bytes 131104 | tf_op jit(solution)/shard_map/ppermute | solution.py:22
  80.3 11.5 %convolution_bitcast_fusion.1 = f32[8,4,8,256]{3,2,1,0:T(8,128)S(1)} fusion(f32[8,9,256,256]{3,2,1,0:T(8,128)S(1)} %multiply_multiply_fusion, f32[32,8,9,256]{3,0,2,1:T(8,128)S(1)} %fusion.27), kind=kOutput, calls=%fused_computation.4 | convolution fusion | flops 1811939328 | bytes 21495808 | tf_op jit(solution)/shard_map/mbkq,bkqp->mbp/dot_general | solution.py:60
  97.4 3.4 %collective-permute-done.7 = f32[32,1024]{1,0:T(8,128)S(1)} collective-permute-done((f32[32,1024]{1,0:T(8,128)S(1)}, f32[32,1024]{1,0:T(8,128)S(1)}, u32[]{:S(2)}, u32[]{:S(2)}) %collective-permute-start.7) | collective-permute-done | bytes 131104 | tf_op jit(solution)/shard_map/ppermute | solution.py:22
  102.0 11.7 %convolution_bitcast_fusion = f32[8,4,8,256]{3,2,1,0:T(8,128)S(1)} fusion(f32[8,9,256,256]{3,2,1,0:T(8,128)S(1)} %multiply_multiply_fusion, f32[32,8,9,256]{3,0,2,1:T(8,128)S(1)} %fusion.18), kind=kOutput, calls=%fused_computation.3 | convolution fusion | flops 1811939328 | bytes 21495808 | tf_op jit(solution)/shard_map/mbkq,bkqp->mbp/dot_general | solution.py:60
  117.7 3.2 %collective-permute-done.10 = f32[128,160]{0,1:T(8,128)S(1)} collective-permute-done((f32[128,160]{0,1:T(8,128)S(1)}, f32[128,160]{0,1:T(8,128)S(1)}, u32[]{:S(2)}, u32[]{:S(2)}) %collective-permute-start.10) | collective-permute-done | bytes 81952 | tf_op jit(solution)/shard_map/ppermute | solution.py:99
  121.4 5.6 %collective-permute-done.11 = f32[128,160]{0,1:T(8,128)S(1)} collective-permute-done((f32[128,160]{0,1:T(8,128)S(1)}, f32[128,160]{0,1:T(8,128)S(1)}, u32[]{:S(2)}, u32[]{:S(2)}) %collective-permute-start.11) | collective-permute-done | bytes 81952 | tf_op jit(solution)/shard_map/ppermute | solution.py:99
  127.1 5.9 %collective-permute-done.12 = f32[128,160]{0,1:T(8,128)S(1)} collective-permute-done((f32[128,160]{0,1:T(8,128)S(1)}, f32[128,160]{0,1:T(8,128)S(1)}, u32[]{:S(2)}, u32[]{:S(2)}) %collective-permute-start.12) | collective-permute-done | bytes 81952 | tf_op jit(solution)/shard_map/ppermute | solution.py:99
  133.1 4.5 %collective-permute-done.13 = f32[128,160]{0,1:T(8,128)S(1)} collective-permute-done((f32[128,160]{0,1:T(8,128)S(1)}, f32[128,160]{0,1:T(8,128)S(1)}, u32[]{:S(2)}, u32[]{:S(2)}) %collective-permute-start.13) | collective-permute-done | bytes 81952 | tf_op jit(solution)/shard_map/ppermute | solution.py:99
  137.7 8.0 %collective-permute-done.14 = f32[128,160]{0,1:T(8,128)S(1)} collective-permute-done((f32[128,160]{0,1:T(8,128)S(1)}, f32[128,160]{0,1:T(8,128)S(1)}, u32[]{:S(2)}, u32[]{:S(2)}) %collective-permute-start.14) | collective-permute-done | bytes 81952 | tf_op jit(solution)/shard_map/ppermute | solution.py:99
  148.0 6.1 %collective-permute-done.15 = f32[128,160]{0,1:T(8,128)S(1)} collective-permute-done((f32[128,160]{0,1:T(8,128)S(1)}, f32[128,160]{0,1:T(8,128)S(1)}, u32[]{:S(2)}, u32[]{:S(2)}) %collective-permute-start.15) | collective-permute-done | bytes 81952 | tf_op jit(solution)/shard_map/ppermute | solution.py:99
  154.2 4.4 %collective-permute-done.16 = f32[128,160]{0,1:T(8,128)S(1)} collective-permute-done((f32[128,160]{0,1:T(8,128)S(1)}, f32[128,160]{0,1:T(8,128)S(1)}, u32[]{:S(2)}, u32[]{:S(2)}) %collective-permute-start.16) | collective-permute-done | bytes 81952 | tf_op jit(solution)/shard_map/ppermute | solution.py:99
  158.8 11.7 %cholesky.44 = f32[128,128]{1,0:T(8,128)S(1)} custom-call(f32[128,128]{1,0:T(8,128)S(1)} %fusion.56), custom_call_target="Cholesky" | custom-call | tf_op jit(solution)/shard_map/jit(cholesky)/cholesky | solution.py:68
  171.9 9.8 %custom-call.10 = f32[1,128,128]{1,2,0:T(8,128)S(1)} custom-call(f32[1,128,128]{2,1,0:T(8,128)S(1)} %fusion.45), custom_call_target="InvertDiagBlocksLowerTriangular" | custom-call | tf_op jit(solution)/shard_map/triangular_solve | solution.py:69
  182.9 11.7 %cholesky.55 = f32[128,128]{1,0:T(8,128)S(1)} custom-call(f32[128,128]{1,0:T(8,128)S(1)} %fusion.52), custom_call_target="Cholesky" | custom-call | tf_op jit(solution)/shard_map/jit(cholesky)/cholesky | solution.py:78
  196.0 10.0 %custom-call.11 = f32[1,128,128]{1,2,0:T(8,128)S(1)} custom-call(f32[1,128,128]{2,1,0:T(8,128)S(1)} %fusion.46), custom_call_target="InvertDiagBlocksLowerTriangular" | custom-call | tf_op jit(solution)/shard_map/triangular_solve | solution.py:80
  216.9 4.4 %collective-permute-done.19 = f32[64,2048]{1,0:T(8,128)S(1)} collective-permute-done((f32[64,2048]{1,0:T(8,128)S(1)}, f32[64,2048]{1,0:T(8,128)S(1)}, u32[]{:S(2)}, u32[]{:S(2)}) %collective-permute-start.19) | collective-permute-done | bytes 524320 | tf_op jit(solution)/shard_map/ppermute | solution.py:28
  (173 shorter events, 46.9 us)
Async XLA Ops:
  0.6 0.8 copy-start
  2.4 17.9 %collective-permute-start = (f32[19,1024]{1,0:T(8,128)S(1)}, f32[19,1024]{1,0:T(8,128)S(1)}, u32[]{:S(2)}, u32[]{:S(2)}) collective-permute-start(f32[19,1024]{1,0:T(8,128)S(1)} %pad_maximum_fusion.10), channel_id=1, source_target_pairs={{0,16},{16,32},{32,48},{48,64},{64,80},{80,96},{96,112},{112,128},... | collective-permute-start | bytes 233480 | tf_op jit(solution)/shard_map/ppermute | solution.py:132
  6.6 29.6 %collective-permute-start.2 = (f32[16,3072]{1,0:T(8,128)S(1)}, f32[16,3072]{1,0:T(8,128)S(1)}, u32[]{:S(2)}, u32[]{:S(2)}) collective-permute-start(f32[16,3072]{1,0:T(8,128)S(1)} %bitcast.374), channel_id=1, source_target_pairs={{0,1},{1,0},{2,3},{3,2},{4,5},{5,4},{6,7},{7,6},{8,9},{9,8},{10,11... | collective-permute-start | bytes 589832 | tf_op jit(solution)/shard_map/ppermute | solution.py:28
  12.6 7.7 %collective-permute-start.1 = (f32[16,1024]{1,0:T(8,128)S(1)}, f32[16,1024]{1,0:T(8,128)S(1)}, u32[]{:S(2)}, u32[]{:S(2)}) collective-permute-start(f32[16,1024]{1,0:T(8,128)S(1)} %bitcast.376), channel_id=1, source_target_pairs={{1,16},{17,32},{33,48},{49,64},{65,80},{81,96},{97,112},{113,128},... | collective-permute-start | bytes 196616 | tf_op jit(solution)/shard_map/ppermute | solution.py:133
  48.4 5.0 %collective-permute-start.4 = (f32[32,1024]{1,0:T(8,128)S(1)}, f32[32,1024]{1,0:T(8,128)S(1)}, u32[]{:S(2)}, u32[]{:S(2)}) collective-permute-start(f32[32,1024]{1,0:T(8,128)S(1)} %get-tuple-element.44), channel_id=1, source_target_pairs={{1,0},{16,1},{17,16},{32,17},{33,32},{48,33},{49,48},{64,49},{65,6... | collective-permute-start | bytes 393224 | tf_op jit(solution)/shard_map/ppermute | solution.py:23
  49.0 8.7 %collective-permute-start.3 = (f32[32,1024]{1,0:T(8,128)S(1)}, f32[32,1024]{1,0:T(8,128)S(1)}, u32[]{:S(2)}, u32[]{:S(2)}) collective-permute-start(f32[32,1024]{1,0:T(8,128)S(1)} %get-tuple-element.43), channel_id=1, source_target_pairs={{0,1},{1,16},{16,17},{17,32},{32,33},{33,48},{48,49},{49,64},{64,6... | collective-permute-start | bytes 393224 | tf_op jit(solution)/shard_map/ppermute | solution.py:22
  70.5 5.2 %collective-permute-start.6 = (f32[32,1024]{1,0:T(8,128)S(1)}, f32[32,1024]{1,0:T(8,128)S(1)}, u32[]{:S(2)}, u32[]{:S(2)}) collective-permute-start(f32[32,1024]{1,0:T(8,128)S(1)} %get-tuple-element.42), channel_id=1, source_target_pairs={{1,0},{16,1},{17,16},{32,17},{33,32},{48,33},{49,48},{64,49},{65,6... | collective-permute-start | bytes 393224 | tf_op jit(solution)/shard_map/ppermute | solution.py:23
  70.8 8.4 %collective-permute-start.5 = (f32[32,1024]{1,0:T(8,128)S(1)}, f32[32,1024]{1,0:T(8,128)S(1)}, u32[]{:S(2)}, u32[]{:S(2)}) collective-permute-start(f32[32,1024]{1,0:T(8,128)S(1)} %get-tuple-element.41), channel_id=1, source_target_pairs={{0,1},{1,16},{16,17},{17,32},{32,33},{33,48},{48,49},{49,64},{64,6... | collective-permute-start | bytes 393224 | tf_op jit(solution)/shard_map/ppermute | solution.py:22
  92.0 5.5 %collective-permute-start.8 = (f32[32,1024]{1,0:T(8,128)S(1)}, f32[32,1024]{1,0:T(8,128)S(1)}, u32[]{:S(2)}, u32[]{:S(2)}) collective-permute-start(f32[32,1024]{1,0:T(8,128)S(1)} %get-tuple-element.40), channel_id=1, source_target_pairs={{1,0},{16,1},{17,16},{32,17},{33,32},{48,33},{49,48},{64,49},{65,6... | collective-permute-start | bytes 393224 | tf_op jit(solution)/shard_map/ppermute | solution.py:23
  92.5 8.4 %collective-permute-start.7 = (f32[32,1024]{1,0:T(8,128)S(1)}, f32[32,1024]{1,0:T(8,128)S(1)}, u32[]{:S(2)}, u32[]{:S(2)}) collective-permute-start(f32[32,1024]{1,0:T(8,128)S(1)} %get-tuple-element.39), channel_id=1, source_target_pairs={{0,1},{1,16},{16,17},{17,32},{32,33},{33,48},{48,49},{49,64},{64,6... | collective-permute-start | bytes 393224 | tf_op jit(solution)/shard_map/ppermute | solution.py:22
  114.9 1.4 collective-permute-start.9
  116.3 4.6 %collective-permute-start.10 = (f32[128,160]{0,1:T(8,128)S(1)}, f32[128,160]{0,1:T(8,128)S(1)}, u32[]{:S(2)}, u32[]{:S(2)}) collective-permute-start(f32[128,160]{0,1:T(8,128)S(1)} %fusion.73), channel_id=1, source_target_pairs={{0,4},{2,6},{4,0},{6,2},{8,12},{10,14},{12,8},{14,10},{1,5},{3,7},... | collective-permute-start | bytes 245768 | tf_op jit(solution)/shard_map/ppermute | solution.py:99
  120.9 6.0 %collective-permute-start.11 = (f32[128,160]{0,1:T(8,128)S(1)}, f32[128,160]{0,1:T(8,128)S(1)}, u32[]{:S(2)}, u32[]{:S(2)}) collective-permute-start(f32[128,160]{0,1:T(8,128)S(1)} %add.126), channel_id=1, source_target_pairs={{0,8},{2,10},{4,12},{6,14},{8,0},{10,2},{12,4},{14,6},{1,9},{3,11}... | collective-permute-start | bytes 245768 | tf_op jit(solution)/shard_map/ppermute | solution.py:99
  127.0 6.0 %collective-permute-start.12 = (f32[128,160]{0,1:T(8,128)S(1)}, f32[128,160]{0,1:T(8,128)S(1)}, u32[]{:S(2)}, u32[]{:S(2)}) collective-permute-start(f32[128,160]{0,1:T(8,128)S(1)} %add.127), channel_id=1, source_target_pairs={{0,16},{16,0},{32,48},{48,32},{64,80},{80,64},{96,112},{112,96},{1... | collective-permute-start | bytes 245768 | tf_op jit(solution)/shard_map/ppermute | solution.py:99
  133.0 4.6 %collective-permute-start.13 = (f32[128,160]{0,1:T(8,128)S(1)}, f32[128,160]{0,1:T(8,128)S(1)}, u32[]{:S(2)}, u32[]{:S(2)}) collective-permute-start(f32[128,160]{0,1:T(8,128)S(1)} %add.128), channel_id=1, source_target_pairs={{0,32},{16,48},{32,0},{48,16},{64,96},{80,112},{96,64},{112,80},{1... | collective-permute-start | bytes 245768 | tf_op jit(solution)/shard_map/ppermute | solution.py:99
  137.6 8.1 %collective-permute-start.14 = (f32[128,160]{0,1:T(8,128)S(1)}, f32[128,160]{0,1:T(8,128)S(1)}, u32[]{:S(2)}, u32[]{:S(2)}) collective-permute-start(f32[128,160]{0,1:T(8,128)S(1)} %add.129), channel_id=1, source_target_pairs={{0,64},{16,80},{32,96},{48,112},{64,0},{80,16},{96,32},{112,48},{1... | collective-permute-start | bytes 245768 | tf_op jit(solution)/shard_map/ppermute | solution.py:99
  145.7 8.4 %collective-permute-start.15 = (f32[128,160]{0,1:T(8,128)S(1)}, f32[128,160]{0,1:T(8,128)S(1)}, u32[]{:S(2)}, u32[]{:S(2)}) collective-permute-start(f32[128,160]{0,1:T(8,128)S(1)} %add.130), channel_id=1, source_target_pairs={{0,128},{16,144},{32,160},{48,176},{64,192},{80,208},{96,224},{112... | collective-permute-start | bytes 245768 | tf_op jit(solution)/shard_map/ppermute | solution.py:99
  154.1 4.5 %collective-permute-start.16 = (f32[128,160]{0,1:T(8,128)S(1)}, f32[128,160]{0,1:T(8,128)S(1)}, u32[]{:S(2)}, u32[]{:S(2)}) collective-permute-start(f32[128,160]{0,1:T(8,128)S(1)} %add.131), channel_id=1, source_target_pairs={{0,1},{1,0},{2,3},{3,2},{4,5},{5,4},{6,7},{7,6},{8,9},{9,8},{10,11... | collective-permute-start | bytes 245768 | tf_op jit(solution)/shard_map/ppermute | solution.py:99
  209.2 5.1 %collective-permute-start.17 = (f32[16,2048]{1,0:T(8,128)S(1)}, f32[16,2048]{1,0:T(8,128)S(1)}, u32[]{:S(2)}, u32[]{:S(2)}) collective-permute-start(f32[16,2048]{1,0:T(8,128)S(1)} %get-tuple-element.38), channel_id=1, source_target_pairs={{0,1},{1,0},{2,3},{3,2},{4,5},{5,4},{6,7},{7,6},{8,9},{9,8},{10,11... | collective-permute-start | bytes 393224 | tf_op jit(solution)/shard_map/ppermute | solution.py:28
  209.4 6.2 %collective-permute-start.18 = (f32[16,2048]{1,0:T(8,128)S(1)}, f32[16,2048]{1,0:T(8,128)S(1)}, u32[]{:S(2)}, u32[]{:S(2)}) collective-permute-start(f32[16,2048]{1,0:T(8,128)S(1)} %get-tuple-element.36), channel_id=1, source_target_pairs={{0,1},{1,0},{2,3},{3,2},{4,5},{5,4},{6,7},{7,6},{8,9},{9,8},{10,11... | collective-permute-start | bytes 393224 | tf_op jit(solution)/shard_map/ppermute | solution.py:28
  211.7 9.6 %collective-permute-start.19 = (f32[64,2048]{1,0:T(8,128)S(1)}, f32[64,2048]{1,0:T(8,128)S(1)}, u32[]{:S(2)}, u32[]{:S(2)}) collective-permute-start(f32[64,2048]{1,0:T(8,128)S(1)} %get-tuple-element.7), channel_id=1, source_target_pairs={{0,1},{1,0},{2,3},{3,2},{4,5},{5,4},{6,7},{7,6},{8,9},{9,8},{10,11... | collective-permute-start | bytes 1572872 | tf_op jit(solution)/shard_map/ppermute | solution.py:28
